TPU v7x, 256 devices: a whole 4x4x8 slice. The times are simulated.
256 devices in a mesh: row: 32 (over x_lo, z, core), feat: 8 (over x_hi, y).
Axes of the slice: x: 4 (x_hi: 2, x_lo: 2; x = x_hi * 2 + x_lo), y: 4, z: 8, core: 2. Of those that a mesh axis runs over, the one named last changes fastest.
Arguments:
- features: bfloat16 [8192, 1024], P('row', 'feat'), may hold values from -6 to 6
- weight: bfloat16 [1024, 1024], P('feat'), may hold values from -0.1875 to 0.1875
- bias_vector: bfloat16 [1024], P('feat'), may hold values from -3 to 3
- adj_tiles: bfloat16 [2048, 128, 128], P('row'), may hold values from -0.09375 to 0.09375
- col_blocks: int32 [2048], P('row'), may hold values from 0 to 63, as said below
- dest_blocks: int32 [2048], P('row'), may hold values from 0 to 1
- out_grad: bfloat16 [8192, 1024], P('row', 'feat'), may hold values from -6 to 6
Outputs:
- hidden: float32 [8192, 1024], P('row', 'feat')
- input_grad: float32 [8192, 1024], P('row', 'feat')
- weight_grad: float32 [1024, 1024], P('feat')
- bias_grad: float32 [1024], P('feat')
Inputs may be any that keep to these rules, and one draw needn't show every extreme that they name: Within the 64 entries of one index r of row, col_blocks // 2 never falls from one entry to the next and is never r; at most 4 of them lie in any one index's range of 2 blocks, and exactly 4 lie in the range of index (r + 1) mod 32.
All inputs are finite; a program needn't handle non-finite values.
Results may differ from a plain program's by a relative error of at most 0.0055.
Values may be sent and summed in bfloat16 or wider, within the bound.
No kernel may reach another device: no remote copies, remote signals or barrier semaphores. Data moves between devices by JAX's collectives and lax.ppermute only.
A program may use at most 64 MiB of HBM per device.

v0:
```python
import jax
import jax.numpy as jnp
from jax import lax
from jax.sharding import PartitionSpec as P


def body(features, weight, bias_vector, adj_tiles, col_blocks, dest_blocks, out_grad):
    cycle_size = lax.axis_size("row")
    block_rows = adj_tiles.shape[1]
    shard_rows = features.shape[0]
    feat_width = features.shape[1]
    local_blocks = shard_rows // block_rows
    tile_count = adj_tiles.shape[0]
    capacity = 2 * tile_count // cycle_size
    owner_index = col_blocks // local_blocks
    highest = lax.Precision.HIGHEST

    def window(first_owner, owners):
        length = min(owners * capacity, tile_count)
        begin_at = jnp.sum((owner_index < first_owner).astype(jnp.int32))
        begin_at = jnp.clip(begin_at, 0, tile_count - length)
        return (begin_at, length, adj_tiles, col_blocks, dest_blocks)

    incoming = lax.all_gather(features, "row", axis=0, tiled=True)
    owners = max(incoming.shape[0] // shard_rows, 1)
    in_blocks = incoming.shape[0] // block_rows
    begin_at, length, tile_slice, col_slice, dest_slice = window(jnp.int32(0) // shard_rows, owners)
    relative = col_slice
    inside = (relative >= 0) & (relative < in_blocks)
    blocks = incoming.reshape(in_blocks, block_rows, feat_width)[
        jnp.clip(relative, 0, in_blocks - 1)
    ]
    blocks = jnp.where(inside[:, None, None], blocks, jnp.zeros_like(blocks))
    begin_at, length, tile_slice, dest_slice, blocks = (
        begin_at,
        length,
        tile_slice,
        dest_slice,
        blocks,
    )
    contrib = jnp.einsum("lij,ljf->lif", tile_slice, blocks, preferred_element_type=jnp.float32)
    onehot = (dest_slice[:, None] == jnp.arange(local_blocks)[None, :]).astype(jnp.float32)
    summed = jnp.einsum("lb,lif->bif", onehot, contrib, precision=highest)
    aggregated = summed.reshape(shard_rows, feat_width).astype(jnp.bfloat16)
    partial_terms = jnp.dot(aggregated, weight, preferred_element_type=jnp.float32)
    preact = lax.psum_scatter(partial_terms, "feat", scatter_dimension=1, tiled=True)
    preact = preact + bias_vector.astype(jnp.float32)
    hidden = jax.nn.silu(preact)
    sigmoid_z = jax.nn.sigmoid(preact)
    grad_pre = (
        out_grad.astype(jnp.float32) * sigmoid_z * (1.0 + preact * (1.0 - sigmoid_z))
    ).astype(jnp.bfloat16)
    incoming = lax.all_gather(grad_pre, "feat", axis=1, tiled=True)
    outer = jnp.einsum("rf,rp->fp", aggregated, incoming, preferred_element_type=jnp.float32)
    weight_part = outer
    prop_part = jnp.einsum("rp,fp->rf", incoming, weight, preferred_element_type=jnp.float32)
    weight_part, prop_part = (weight_part, prop_part)
    bias_part = jnp.sum(grad_pre.astype(jnp.float32), axis=0)
    weight_total, bias_total = lax.psum((weight_part, bias_part), "row")
    grad_scale = float(shard_rows * cycle_size) ** (-0.5)
    weight_grad = weight_total * grad_scale
    bias_grad = bias_total * grad_scale
    prop_grad = prop_part.astype(jnp.bfloat16)
    prop_blocks = prop_grad.reshape(local_blocks, block_rows, feat_width)
    owners = shard_rows * lax.axis_size("row") // shard_rows
    out_blocks = shard_rows * lax.axis_size("row") // block_rows
    begin_at, length, tile_slice, col_slice, dest_slice = window(jnp.int32(0) // shard_rows, owners)
    relative = col_slice
    gathered = prop_blocks[dest_slice]
    contrib = jnp.einsum("lij,lif->ljf", tile_slice, gathered, preferred_element_type=jnp.float32)
    onehot = (relative[:, None] == jnp.arange(out_blocks)[None, :]).astype(jnp.float32)
    placed = jnp.einsum("lk,ljf->kjf", onehot, contrib, precision=highest)
    input_grad = lax.psum_scatter(
        placed.reshape(shard_rows * lax.axis_size("row"), feat_width),
        "row",
        scatter_dimension=0,
        tiled=True,
    )
    return (hidden, input_grad, weight_grad, bias_grad)


def solution(mesh):
    in_specs = (
        P("row", "feat"),
        P("feat", None),
        P("feat"),
        P("row", None, None),
        P("row"),
        P("row"),
        P("row", "feat"),
    )
    out_specs = (P("row", "feat"), P("row", "feat"), P("feat", None), P("feat"))
    return jax.shard_map(body, mesh=mesh, in_specs=in_specs, out_specs=out_specs, check_vma=False)
```

profile of v0, /device:TPU:1, one launch (start us, length us, event | category | flops | bytes accessed | tf_op | source)
XLA Modules:
  0.0 555.5 jit_solution(2048435504981622855)
XLA Ops:
  7.2 0.0 copy-start
  7.2 0.0 all-gather.2.cloned.1.call-start
  7.2 0.7 all-gather.2.cloned.1.call-update
  7.9 0.0 reduce-scatter.3.cloned.1.call-start
  8.0 0.7 compare_select_fusion.1
  8.6 0.7 compare_and_fusion
  9.3 69.5 %all-gather.2.cloned.1.call-done = bf16[8192,128]{1,0:T(8,128)(2,1)} async-done(((bf16[256,128]{1,0:T(8,128)(2,1)}), bf16[8192,128]{1,0:T(8,128)(2,1)}) %all-gather.2.cloned.1.call-update) | async-done | bytes 2097168 | tf_op jit(solution)/shard_map/all_gather | solution.py:24
  78.8 3.7 gather_fusion
  82.5 0.0 copy-done
  82.5 5.3 fusion.4
  87.8 0.0 copy-start.3
  87.8 5.4 copy.13
  93.2 0.0 copy-done.3
  93.2 0.0 copy-start.1
  93.2 3.7 fusion.7
  96.9 0.0 copy-start.5
  96.9 0.0 copy-start.2
  97.0 0.0 copy-done.1
  97.0 1.2 fusion.20
  98.2 0.0 reduce-scatter.3.cloned.1.call-update
  98.2 0.0 all-reduce.2.cloned.1.call-start
  98.3 0.0 copy-done.5
  98.3 74.2 %reduce-scatter.3.cloned.1.call-done = f32[256,128]{1,0:T(8,128)} async-done(((f32[256,1024]{1,0:T(8,128)}), f32[256,128]{1,0:T(8,128)}) %reduce-scatter.3.cloned.1.call-update) | async-done | bytes 131088 | tf_op jit(solution)/shard_map/reduce_scatter | solution.py:46
  172.6 0.0 copy-done.2
  172.6 1.6 convert_reduce_fusion
  174.2 27.1 %all_gather.7 = bf16[256,1024]{1,0:T(8,128)(2,1)S(1)} all-gather(bf16[256,128]{1,0:T(8,128)(2,1)S(1)} %get-tuple-element.5), channel_id=1, replica_groups=mesh['row'=32,'feat'=8] {'feat'}, dimensions={1}, use_global_device_ids=true | all-gather | bytes 589824 | tf_op jit(solution)/shard_map/all_gather | solution.py:53
  201.3 0.3 convolution_convert_fusion
  201.6 1.1 fusion.22
  202.7 0.0 all-reduce.2.cloned.1.call-update
  202.7 0.0 reduce-scatter.5.cloned.1.call-start
  202.8 2.1 gather_fusion.1
  204.9 4.4 fusion.21
  209.3 0.0 copy-start.4
  209.3 5.4 copy.14
  214.7 0.0 copy-done.4
  214.7 4.6 fusion
  219.3 4.4 copy.12
  223.7 0.0 reduce-scatter.5.cloned.1.call-update
  223.7 58.8 %psum.15 = f32[128]{0:T(128)S(1)} all-reduce(f32[128]{0:T(128)S(1)} %get-tuple-element.4), channel_id=1, replica_groups=mesh['row'=32,'feat'=8] {'row'}, use_global_device_ids=true, to_apply=%region_4.5 | all-reduce | flops 128 | bytes 1024 | tf_op jit(solution)/shard_map/psum | solution.py:59
  282.5 0.5 broadcast_multiply_fusion.1
  283.0 146.2 %all-reduce.2.cloned.1.call-done = f32[128,1024]{1,0:T(8,128)} async-done(((f32[128,1024]{1,0:T(8,128)}), f32[128,1024]{1,0:T(8,128)}) %all-reduce.2.cloned.1.call-update) | async-done | bytes 524304 | tf_op jit(solution)/shard_map/psum | solution.py:59
  429.2 1.9 broadcast_multiply_fusion
  431.0 117.9 %reduce-scatter.5.cloned.1.call-done = f32[256,128]{1,0:T(8,128)} async-done(((f32[8192,128]{1,0:T(8,128)}), f32[256,128]{1,0:T(8,128)}) %reduce-scatter.5.cloned.1.call-update) | async-done | bytes 131088 | tf_op jit(solution)/shard_map/reduce_scatter | solution.py:73
  (5 shorter events, 0.0 us)
Async XLA Ops:
  7.2 75.3 %copy-start = (bf16[64,128,128]{2,1,0:T(8,128)(2,1)S(1)}, bf16[64,128,128]{2,1,0:T(8,128)(2,1)}, u32[]{:S(2)}) copy-start(bf16[64,128,128]{2,1,0:T(8,128)(2,1)} %param.10) | copy-start | bytes 6291460
  7.2 71.6 %all-gather.2.cloned.1.call-start = ((), (), s32[]{:S(2)}) async-start(), calls=%async_computation.2 | async-start | bytes 2162688 | tf_op jit(solution)/shard_map/all_gather | solution.py:24
  7.9 164.7 %reduce-scatter.3.cloned.1.call-start = ((), (), s32[]{:S(2)}) async-start(), calls=%async_computation.3 | async-start | bytes 1179648 | tf_op jit(solution)/shard_map/reduce_scatter | solution.py:46
  87.8 5.4 copy-start.3
  93.2 3.7 copy-start.1
  96.9 1.4 copy-start.5
  96.9 75.7 %copy-start.2 = (bf16[256,128]{1,0:T(8,128)(2,1)S(1)}, bf16[256,128]{1,0:T(8,128)(2,1)}, u32[]{:S(2)}) copy-start(bf16[256,128]{1,0:T(8,128)(2,1)} %param.13) | copy-start | bytes 196612
  98.2 330.9 %all-reduce.2.cloned.1.call-start = ((), (), s32[]{:S(2)}) async-start(), calls=%async_computation.5 | async-start | bytes 1048576 | tf_op jit(solution)/shard_map/psum | solution.py:59
  202.7 346.2 %reduce-scatter.5.cloned.1.call-start = ((), (), s32[]{:S(2)}) async-start(), calls=%async_computation.4 | async-start | bytes 4325376 | tf_op jit(solution)/shard_map/reduce_scatter | solution.py:73
  209.3 5.4 copy-start.4
Sparse Core Ops, SparseCore 0:
  9.9 68.8 all-gather.1
  98.4 74.1 reduce-scatter.2
  202.8 226.2 all-reduce.1
  432.1 116.7 reduce-scatter.4
where the time goes:
time: 559 us; the launch traced here: 555 us
  waiting for transfers between devices  409 us (73%)
  blocking collectives  85.9 us (15%)
  local copies, waits for them, and re-layouts  21.1 us (4%)
  matrix products  20.6 us (4%)
  between operations  13.9 us (2%)
    psum x1, waiting for transfers between devices, body(): weight_total, bias_total = lax.psum((weight_part, bias_part), 'row')  146 us
    reduce_scatter x1, waiting for transfers between devices, body(): lax.psum_scatter(placed.reshape(shard_rows * lax.axis_size('row'), feat_w...  118 us
    reduce_scatter x1, waiting for transfers between devices, body(): lax.psum_scatter(partial_terms, 'feat', scatter_dimension=1, tiled=True)  74.2 us
    all_gather x1, waiting for transfers between devices, body(): incoming = lax.all_gather(features, 'row', axis=0, tiled=True)  69.5 us
    psum x1, blocking collectives, body(): weight_total, bias_total = lax.psum((weight_part, bias_part), 'row')  58.8 us
    all_gather x1, blocking collectives, body(): incoming = lax.all_gather(grad_pre, 'feat', axis=1, tiled=True)  27.1 us
  transfers between devices with their start and end apart: 4, of which 4 were waited for; matrix products, arithmetic and copies ran while one was open for 4% of the time, Pallas kernels for 0%

commit v1 on v0

v1 whole, which is shorter than its diff:
```python
import functools

import jax
import jax.numpy as jnp
from jax import lax
from jax.experimental import pallas as pl
from jax.experimental.pallas import tpu as pltpu
from jax.sharding import PartitionSpec as P

bf16 = jnp.bfloat16
f32 = jnp.float32
B = 128
NZ = 8
VM = pl.BlockSpec(memory_space=pltpu.VMEM)
SM = pl.BlockSpec(memory_space=pltpu.SMEM)


def row_send(v, dx=0, dz=0, dc=0):
    perm = []
    for i in range(32):
        x, z, c = i >> 4, (i >> 1) & 7, i & 1
        perm.append((i, ((x ^ dx) << 4) | (((z + dz) % NZ) << 1) | (c ^ dc)))
    return lax.ppermute(v, "row", perm)


def feat_send(v, dx=0, dy=0):
    return lax.ppermute(v, "feat", [(i, (((i >> 2) ^ dx) << 2) | ((i + dy) & 3)) for i in range(8)])


def params(mib=48):
    return pltpu.CompilerParams(vmem_limit_bytes=mib << 20)


def cost(flops, nbytes):
    return pl.CostEstimate(flops=flops, bytes_accessed=nbytes, transcendentals=0)


def agg_body(idx, dest, tiles, near, far, out):
    group = 4

    def step(g, acc):
        lhs, rhs = [], []
        for u in range(group):
            t = g * group + u
            a = tiles[t]
            zero = jnp.zeros_like(a)
            d = dest[t]
            lhs.append(jnp.concatenate([jnp.where(d == 0, a, zero), jnp.where(d == 1, a, zero)], axis=0))
            i = idx[t]
            j = i & 31
            rhs.append(jnp.where(i < 32, near[j], far[j]))
        return acc + jnp.dot(
            jnp.concatenate(lhs, axis=1), jnp.concatenate(rhs, axis=0), preferred_element_type=f32
        )

    acc = lax.fori_loop(0, 64 // group, step, jnp.zeros((2 * B, B), f32))
    out[...] = acc.astype(bf16)


def aggregate(idx, dest, tiles, near, far):
    return pl.pallas_call(
        agg_body,
        out_shape=jax.ShapeDtypeStruct((2 * B, B), bf16),
        in_specs=[SM, SM, VM, VM, VM],
        out_specs=VM,
        compiler_params=params(),
        cost_estimate=cost(2 * 64 * B**3, 4 << 20),
        name="aggregate",
    )(idx, dest, tiles, near, far)


def lay_body(who, *refs):
    own, other = refs[0:4], refs[4:8]
    w_out, og_out, bias_out = refs[8:11]
    core = who[0]
    for j in range(4):
        for i in range(2):
            k = j * 2 + i
            base = i * 784
            col = pl.multiple_of(who[1 + k] * B, B)
            for src, c in ((own[j], core), (other[j], 1 - core)):
                for m in range(4):
                    at = pl.multiple_of(c * 512 + m * B, B)
                    w_out[pl.ds(k * B, B), pl.ds(at, B)] = src[pl.ds(base + m * B, B), :]
            og_out[:, pl.ds(col, B)] = own[j][pl.ds(base + 512, 256), :]
            bias_out[:, pl.ds(col, B)] = own[j][pl.ds(base + 768, 16), :].astype(f32)[0:8]


def lay_out(who, own, other):
    return pl.pallas_call(
        lay_body,
        out_shape=(
            jax.ShapeDtypeStruct((1024, 1024), bf16),
            jax.ShapeDtypeStruct((256, 1024), bf16),
            jax.ShapeDtypeStruct((8, 1024), f32),
        ),
        in_specs=[SM] + [VM] * 8,
        out_specs=(VM, VM, VM),
        compiler_params=params(),
        cost_estimate=cost(0, 5 << 20),
        name="lay_out",
    )(who, *own, *other)


def mid_body(who, p0, p1, p2, p3, w_full, og, bias, w_own, hidden, prop, wpart, agg, pre, gp):
    for j, p in enumerate((p0, p1, p2, p3)):
        for i in range(2):
            agg[:, (j * 2 + i) * B : (j * 2 + i + 1) * B] = p[i * 256 : (i + 1) * 256, :]
    for n in range(4):
        cols = slice(n * 256, (n + 1) * 256)
        v = jnp.dot(agg[...], w_full[:, cols], preferred_element_type=f32) + bias[0:1, cols]
        pre[:, cols] = v
        s = jax.nn.sigmoid(v)
        gp[:, cols] = (og[:, cols].astype(f32) * s * (1.0 + v * (1.0 - s))).astype(bf16)
    mine = pl.ds(pl.multiple_of(who[0] * B, B), B)
    v = pre[:, mine]
    hidden[...] = v * jax.nn.sigmoid(v)
    prop[...] = lax.dot_general(
        gp[...], w_own[...], (((1,), (1,)), ((), ())), preferred_element_type=f32
    ).astype(bf16)
    wpart[:, 0:1024] = lax.dot_general(
        agg[:, 0:B], gp[...], (((0,), (0,)), ((), ())), preferred_element_type=f32
    )
    total = jnp.sum(gp[:, mine].astype(f32), axis=0, keepdims=True)
    wpart[:, 1024:1152] = jnp.broadcast_to(total, (B, B))


def middle(feat, pieces, w_full, og, bias, w_own):
    return pl.pallas_call(
        mid_body,
        out_shape=(
            jax.ShapeDtypeStruct((256, B), f32),
            jax.ShapeDtypeStruct((256, B), bf16),
            jax.ShapeDtypeStruct((B, 1152), f32),
        ),
        in_specs=[SM] + [VM] * 8,
        out_specs=(VM, VM, VM),
        scratch_shapes=[
            pltpu.VMEM((256, 1024), bf16),
            pltpu.VMEM((256, 1024), f32),
            pltpu.VMEM((256, 1024), bf16),
        ],
        compiler_params=params(),
        cost_estimate=cost(2 * 256 * 1024 * 1280, 5 << 20),
        name="middle",
    )(feat, *pieces, w_full, og, bias, w_own)


def spread_body(idx, dest, tiles, prop, mine, other, acc):
    acc[...] = jnp.zeros_like(acc)

    def step(g, carry):
        for u in range(4):
            t = g * 4 + u
            i = idx[t]
            acc[i] += lax.dot_general(
                tiles[t], prop[dest[t]], (((0,), (0,)), ((), ())), preferred_element_type=f32
            )
        return carry

    lax.fori_loop(0, 16, step, 0)
    mine[...] = acc[0:32]
    other[...] = acc[32:64].astype(bf16)


def spread(idx, dest, tiles, prop):
    return pl.pallas_call(
        spread_body,
        out_shape=(
            jax.ShapeDtypeStruct((32, B, B), f32),
            jax.ShapeDtypeStruct((32, B, B), bf16),
        ),
        in_specs=[SM, SM, VM, VM],
        out_specs=(VM, VM),
        scratch_shapes=[pltpu.VMEM((64, B, B), f32)],
        compiler_params=params(),
        cost_estimate=cost(2 * 64 * B**3, 6 << 20),
        name="spread",
    )(idx, dest, tiles, prop)


def body(features, weight, bias_vector, adj_tiles, col_blocks, dest_blocks, out_grad):
    me = lax.axis_index("row")
    my_x, my_z, my_c = me >> 4, (me >> 1) & 7, me & 1
    ft = lax.axis_index("feat")
    owner = col_blocks >> 1
    ox, oz, oc = owner >> 4, (owner >> 1) & 7, owner & 1
    idx = ((((oc ^ my_c) * NZ + ((oz - my_z) & 7)) * 2 + (ox ^ my_x)) * 2) + (col_blocks & 1)

    half = lax.dynamic_slice(weight, (0, my_c * 512), (B, 512))
    pack = jnp.concatenate(
        [half[:, m * B : (m + 1) * B] for m in range(4)]
        + [out_grad, jnp.broadcast_to(bias_vector[None, :], (16, B))],
        axis=0,
    )
    pair = jnp.concatenate([pack, feat_send(pack, dx=1)], axis=0)
    own = (pair, feat_send(pair, dy=1), feat_send(pair, dy=-1), feat_send(pair, dy=2))
    other = tuple(row_send(p, dc=1) for p in own)
    yy, xx = ft & 3, ft >> 2
    at = [((xx ^ i) << 2) | ((yy + off) & 3) for off in (0, -1, 1, 2) for i in range(2)]
    who = jnp.stack([my_c] + at).astype(jnp.int32)
    w_full, og, bias = lay_out(who, own, other)

    b = jnp.concatenate([features, row_send(features, dx=1)], axis=0)
    got = {0: b}
    up = down = b
    for s in range(1, 5):
        up = row_send(up, dz=1)
        got[NZ - s] = up
        if s < 4:
            down = row_send(down, dz=-1)
            got[s] = down
    near = jnp.concatenate([got[k] for k in range(NZ)], axis=0)
    far = row_send(near, dc=1)
    near, far = near.reshape(32, B, B), far.reshape(32, B, B)

    aggregated = aggregate(idx, dest_blocks, adj_tiles, near, far)

    q = jnp.concatenate([aggregated, feat_send(aggregated, dx=1)], axis=0)
    pieces = (q, feat_send(q, dy=1), feat_send(q, dy=-1), feat_send(q, dy=2))
    hidden, prop, wpart = middle(ft[None].astype(jnp.int32), pieces, w_full, og, bias, weight)

    keep = lax.dynamic_slice(wpart, (my_c * 64, 0), (64, 1152))
    give = lax.dynamic_slice(wpart, ((1 - my_c) * 64, 0), (64, 1152))
    keep = keep + row_send(give, dc=1)
    give = lax.dynamic_slice(keep, ((1 - my_x) * 32, 0), (32, 1152)).astype(bf16)
    keep = lax.dynamic_slice(keep, (my_x * 32, 0), (32, 1152))
    keep = (keep + row_send(give, dx=1).astype(f32)).astype(bf16)

    mine, other = spread(idx, dest_blocks, adj_tiles, prop.reshape(2, B, B))
    part = mine + row_send(other, dc=1).astype(f32)
    part = part.reshape(NZ, 2, 256, B)
    sent = row_send(part[:, 1].astype(bf16), dx=1)
    part = part[:, 0] + sent.astype(f32)
    out = part[0]
    low = part.astype(bf16)

    parts = [keep]
    gup = gdown = keep
    for s in range(1, 5):
        gup = row_send(gup, dz=1)
        parts.append(gup)
        if s < 4:
            gdown = row_send(gdown, dz=-1)
            parts.append(gdown)
    order = jnp.array([0, 2, 4, 6, 7, 5, 3, 1], jnp.int32)
    stacked = jnp.stack(parts)
    total = jnp.zeros((32, 1152), f32)
    for z in range(NZ):
        total = total + lax.dynamic_index_in_dim(
            stacked, order[(z - my_z) & 7], 0, keepdims=False
        ).astype(f32)

    for k in (4, 3, 5, 2, 6, 1, 7):
        out = out + row_send(low[k], dz=k).astype(f32)

    grad_scale = float(256 * lax.axis_size("row")) ** (-0.5)
    total = (total * grad_scale).astype(bf16)
    theirs = row_send(total, dx=1)
    first = jnp.where(my_x == 0, total, theirs)
    second = jnp.where(my_x == 0, theirs, total)
    two = jnp.concatenate([first, second], axis=0)
    theirs = row_send(two, dc=1)
    first = jnp.where(my_c == 0, two, theirs)
    second = jnp.where(my_c == 0, theirs, two)
    whole = jnp.concatenate([first, second], axis=0).astype(f32)
    return hidden, out, whole[:, :1024], whole[0, 1024:]


def solution(mesh):
    in_specs = (
        P("row", "feat"),
        P("feat", None),
        P("feat"),
        P("row", None, None),
        P("row"),
        P("row"),
        P("row", "feat"),
    )
    out_specs = (P("row", "feat"), P("row", "feat"), P("feat", None), P("feat"))
    return jax.shard_map(body, mesh=mesh, in_specs=in_specs, out_specs=out_specs, check_vma=False)
```

time: 559 us -> 192 us (0.34)
  waiting for transfers between devices: 409 us -> 50.5 us
  blocking collectives: 85.9 us -> 0 us
  starting transfers between devices: 0.16 us -> 78.1 us
  matrix products: 20.6 us -> 0 us
  Pallas kernels: 0 us -> 15.5 us
    reduce_scatter x2 -> x0, waiting for transfers between devices: 192 us -> none  [the longest x1 118 us: body(): lax.psum_scatter(placed.reshape(shard_rows * lax.axis_size('row'), feat_w...]
    psum x1 -> x0, waiting for transfers between devices: 146 us -> none  [body(): weight_total, bias_total = lax.psum((weight_part, bias_part), 'row')]
    ppermute x0 -> x41, starting transfers between devices: none -> 78.1 us  [the longest x33 65.7 us: row_send(): return lax.ppermute(v, 'row', perm)]
    all_gather x1 -> x0, waiting for transfers between devices: 69.5 us -> none  [body(): incoming = lax.all_gather(features, 'row', axis=0, tiled=True)]
    psum x1 -> x0, blocking collectives: 58.8 us -> none  [body(): weight_total, bias_total = lax.psum((weight_part, bias_part), 'row')]
    ppermute x0 -> x41, waiting for transfers between devices: none -> 50.5 us  [the longest x33 35.7 us: row_send(): return lax.ppermute(v, 'row', perm)]
    all_gather x1 -> x0, blocking collectives: 27.1 us -> none  [body(): incoming = lax.all_gather(grad_pre, 'feat', axis=1, tiled=True)]
    dot_general x7 -> x0, matrix products: 20.6 us -> none  [the longest x1 5.3 us: body(): jnp.einsum('lij,ljf->lif', tile_slice, blocks, preferred_element_type=jnp...]
  transfers between devices with their start and end apart: 4 -> 41, of which waited for: 4 -> 20; matrix products, arithmetic and copies ran while one was open for 4% -> 8% of each run, Pallas kernels for 0% -> 7%
where the time goes in v1:
time: 192 us; the launch traced here: 189 us
  starting transfers between devices  78.1 us (41%)
  waiting for transfers between devices  50.5 us (26%)
  local copies, waits for them, and re-layouts  21 us (11%)
  between operations  16.1 us (8%)
  Pallas kernels  15.5 us (8%)
  other arithmetic  8.36 us (4%)
    ppermute x33, starting transfers between devices, row_send(): return lax.ppermute(v, 'row', perm)  65.7 us
    ppermute x33, waiting for transfers between devices, row_send(): return lax.ppermute(v, 'row', perm)  35.7 us
    unnamed x51, local copies, waits for them, and re-layouts  17 us
    ppermute x8, waiting for transfers between devices, feat_send(): lax.ppermute(v, 'feat', [(i, (i >> 2 ^ dx) << 2 | i + dy & 3) for i in ra...  14.7 us
    ppermute x8, starting transfers between devices, feat_send(): lax.ppermute(v, 'feat', [(i, (i >> 2 ^ dx) << 2 | i + dy & 3) for i in ra...  12.4 us
    pallas_call x1, Pallas kernels, spread(): pl.pallas_call(spread_body, out_shape=(jax.ShapeDtypeStruct((32, B, B), f...  5.55 us
    pallas_call x1, Pallas kernels, aggregate(): pl.pallas_call(agg_body, out_shape=jax.ShapeDtypeStruct((2 * B, B), bf16)...  5.15 us
  transfers between devices with their start and end apart: 41, of which 20 were waited for; matrix products, arithmetic and copies ran while one was open for 8% of the time, Pallas kernels for 7%

profile of v1, /device:TPU:1, one launch (start us, length us, event | category | flops | bytes accessed | tf_op | source)
XLA Modules:
  0.0 189.5 jit_solution(10110069104010217754)
XLA Ops:
  0.7 2.1 %collective-permute-start = (bf16[256,128]{1,0:T(8,128)(2,1)}, bf16[256,128]{1,0:T(8,128)(2,1)S(1)}, u32[]{:S(2)}, u32[]{:S(2)}) collective-permute-start(bf16[256,128]{1,0:T(8,128)(2,1)} %param.8), channel_id=1, source_target_pairs={{0,128},{8,136},{16,144},{24,152},{32,160},{40,168},{48,176},{56,1... | collective-permute-start | bytes 196616 | tf_op jit(solution)/shard_map/ppermute | solution.py:23
  2.8 1.5 constant_dynamic-update-slice_fusion.1
  7.3 1.6 collective-permute-start.4
  9.0 1.4 constant_dynamic-update-slice_fusion.13
  10.4 3.9 %collective-permute-start.1 = (bf16[512,128]{1,0:T(8,128)(2,1)}, bf16[512,128]{1,0:T(8,128)(2,1)S(1)}, u32[]{:S(2)}, u32[]{:S(2)}) collective-permute-start(bf16[512,128]{1,0:T(8,128)(2,1)} %get-tuple-element.39), channel_id=1, source_target_pairs={{0,112},{8,120},{16,0},{24,8},{32,16},{40,24},{48,32},{56,40},{64,... | collective-permute-start | bytes 393224 | tf_op jit(solution)/shard_map/ppermute | solution.py:23
  16.8 2.7 %collective-permute-start.2 = (bf16[512,128]{1,0:T(8,128)(2,1)S(1)}, bf16[512,128]{1,0:T(8,128)(2,1)S(1)}, u32[]{:S(2)}, u32[]{:S(2)}) collective-permute-start(bf16[512,128]{1,0:T(8,128)(2,1)S(1)} %collective-permute-done.1), channel_id=1, source_target_pairs={{0,112},{8,120},{16,0},{24,8},{32,16},{40,24},{48,32},{56,40},{64,... | collective-permute-start | bytes 393224 | tf_op jit(solution)/shard_map/ppermute | solution.py:23
  21.1 1.5 constant_dynamic-update-slice_fusion.12
  22.5 2.7 %collective-permute-start.3 = (bf16[512,128]{1,0:T(8,128)(2,1)S(1)}, bf16[512,128]{1,0:T(8,128)(2,1)S(1)}, u32[]{:S(2)}, u32[]{:S(2)}) collective-permute-start(bf16[512,128]{1,0:T(8,128)(2,1)S(1)} %collective-permute-done.2), channel_id=1, source_target_pairs={{0,112},{8,120},{16,0},{24,8},{32,16},{40,24},{48,32},{56,40},{64,... | collective-permute-start | bytes 393224 | tf_op jit(solution)/shard_map/ppermute | solution.py:23
  27.2 3.9 %collective-permute-done.7 = bf16[512,128]{1,0:T(8,128)(2,1)S(1)} collective-permute-done((bf16[512,128]{1,0:T(8,128)(2,1)S(1)}, bf16[512,128]{1,0:T(8,128)(2,1)S(1)}, u32[]{:S(2)}, u32[]{:S(2)}) %collective-permute-start.7) | collective-permute-done | bytes 131104 | tf_op jit(solution)/shard_map/ppermute | solution.py:23
  31.2 5.1 %collective-permute-start.8 = (bf16[4096,128]{1,0:T(8,128)(2,1)S(1)}, bf16[4096,128]{1,0:T(8,128)(2,1)}, u32[]{:S(2)}, u32[]{:S(2)}) collective-permute-start(bf16[4096,128]{1,0:T(8,128)(2,1)S(1)} %constant_dynamic-update-slice_fusion.2), channel_id=1, source_target_pairs={{0,8},{8,0},{16,24},{24,16},{32,40},{40,32},{48,56},{56,48},{64,72... | collective-permute-start | bytes 3145736 | tf_op jit(solution)/shard_map/ppermute | solution.py:23
  36.9 2.5 %collective-permute-start.13 = (bf16[784,128]{1,0:T(8,128)(2,1)}, bf16[784,128]{1,0:T(8,128)(2,1)S(1)}, u32[]{:S(2)}, u32[]{:S(2)}) collective-permute-start(bf16[784,128]{1,0:T(8,128)(2,1)} %get-tuple-element.51), channel_id=1, source_target_pairs={{0,4},{1,5},{2,6},{3,7},{4,0},{5,1},{6,2},{7,3},{8,12},{9,13},{10,... | collective-permute-start | bytes 602120 | tf_op jit(solution)/shard_map/ppermute | solution.py:27
  39.3 5.9 %collective-permute-done.13 = bf16[784,128]{1,0:T(8,128)(2,1)S(1)} collective-permute-done((bf16[784,128]{1,0:T(8,128)(2,1)}, bf16[784,128]{1,0:T(8,128)(2,1)S(1)}, u32[]{:S(2)}, u32[]{:S(2)}) %collective-permute-start.13) | collective-permute-done | bytes 200736 | tf_op jit(solution)/shard_map/ppermute | solution.py:27
  45.2 1.4 collective-permute-start.14
  46.6 1.5 collective-permute-start.15
  48.1 1.6 collective-permute-start.16
  49.7 1.6 collective-permute-start.17
  51.3 5.4 %collective-permute-done.14.refs_1_ = bf16[1568,128]{1,0:T(8,128)(2,1)} collective-permute-done((bf16[1568,128]{1,0:T(8,128)(2,1)S(1)}, bf16[1568,128]{1,0:T(8,128)(2,1)}, u32[]{:S(2)}, u32[]{:S(2)}) %collective-permute-start.14) | collective-permute-done | bytes 401440 | tf_op jit(solution)/shard_map/ppermute | solution.py:27
  56.8 1.7 collective-permute-start.18
  58.5 7.8 %collective-permute-start.19 = (bf16[1568,128]{1,0:T(8,128)(2,1)}, bf16[1568,128]{1,0:T(8,128)(2,1)}, u32[]{:S(2)}, u32[]{:S(2)}) collective-permute-start(bf16[1568,128]{1,0:T(8,128)(2,1)} %collective-permute-done.15.refs_2_), channel_id=1, source_target_pairs={{0,8},{8,0},{16,24},{24,16},{32,40},{40,32},{48,56},{56,48},{64,72... | collective-permute-start | bytes 1204232 | tf_op jit(solution)/shard_map/ppermute | solution.py:23
  66.5 1.7 collective-permute-start.20
  68.9 5.2 %aggregate.1 = bf16[256,128]{1,0:T(8,128)(2,1)S(1)} custom-call(s32[64]{0:T(128)S(1)} %and_add_fusion.idx, s32[64]{0:T(128)S(1)} %copy-done.10, bf16[64,128,128]{2,1,0:T(8,128)(2,1)S(1)} %copy-done, bf16[32,128,128]{2,1,0:T(8,128)(2,1)S(1)} %bitcast.81, bf16[32,128,128]{2,1,0:T(8,128)(2,1)} %bitcast.2.far), custom_call_target="tpu_custom_call" | custom-call | flops 268435456 | bytes 4194304 | tf_op jit(solution)/shard_map/aggregate/pallas_call | solution.py:61
  74.0 2.7 %collective-permute-start.9 = (bf16[256,128]{1,0:T(8,128)(2,1)S(1)}, bf16[256,128]{1,0:T(8,128)(2,1)S(1)}, u32[]{:S(2)}, u32[]{:S(2)}) collective-permute-start(bf16[256,128]{1,0:T(8,128)(2,1)S(1)} %aggregate.1), channel_id=1, source_target_pairs={{0,4},{1,5},{2,6},{3,7},{4,0},{5,1},{6,2},{7,3},{8,12},{9,13},{10,... | collective-permute-start | bytes 196616 | tf_op jit(solution)/shard_map/ppermute | solution.py:27
  76.7 2.8 %collective-permute-done.9 = bf16[256,128]{1,0:T(8,128)(2,1)S(1)} collective-permute-done((bf16[256,128]{1,0:T(8,128)(2,1)S(1)}, bf16[256,128]{1,0:T(8,128)(2,1)S(1)}, u32[]{:S(2)}, u32[]{:S(2)}) %collective-permute-start.9) | collective-permute-done | bytes 65568 | tf_op jit(solution)/shard_map/ppermute | solution.py:27
  81.2 1.8 collective-permute-start.11
  85.9 2.2 %lay_out.1 = (bf16[1024,1024]{1,0:T(8,128)(2,1)S(1)}, bf16[256,1024]{1,0:T(8,128)(2,1)S(1)}, f32[8,1024]{1,0:T(8,128)S(1)}) custom-call(s32[9]{0:T(128)S(1)} %stack.66.who, bf16[1568,128]{1,0:T(8,128)(2,1)S(1)} %constant_dynamic-update-slice_fusion.17.refs_0_, bf16[1568,128]{1,0:T(8,128)(2,1)} %collective-permute-done.14.refs_1_, ...), custom_call_target="tpu_custom_call" | custom-call | bytes 5242880 | tf_op jit(solution)/shard_map/lay_out/pallas_call | solution.py:90
  90.2 2.6 %middle.1 = (f32[256,128]{1,0:T(8,128)}, bf16[256,128]{1,0:T(8,128)(2,1)S(1)}, f32[128,1152]{1,0:T(8,128)S(1)}) custom-call(s32[1]{0:T(128)} %bitcast.who, bf16[512,128]{1,0:T(8,128)(2,1)S(1)} %pad_maximum_fusion.1.p0, bf16[512,128]{1,0:T(8,128)(2,1)S(1)} %copy-done.9, bf16[512,128]{1,0:T(8,128)(2,1)} %collective-permute-done.11.p2, ...), custom_call_target="tpu_custom_call" | custom-call | flops 671088640 | bytes 5242880 | tf_op jit(solution)/shard_map/middle/pallas_call | solution.py:129
  92.8 2.6 %collective-permute-start.30 = (f32[64,1152]{1,0:T(8,128)S(1)}, f32[64,1152]{1,0:T(8,128)S(1)}, u32[]{:S(2)}, u32[]{:S(2)}) collective-permute-start(f32[64,1152]{1,0:T(8,128)S(1)} %constant_dynamic-slice_fusion), channel_id=1, source_target_pairs={{0,8},{8,0},{16,24},{24,16},{32,40},{40,32},{48,56},{56,48},{64,72... | collective-permute-start | bytes 884744 | tf_op jit(solution)/shard_map/ppermute | solution.py:23
  98.7 2.8 %collective-permute-done.31 = bf16[32,1152]{1,0:T(8,128)(2,1)S(1)} collective-permute-done((bf16[32,1152]{1,0:T(8,128)(2,1)S(1)}, bf16[32,1152]{1,0:T(8,128)(2,1)S(1)}, u32[]{:S(2)}, u32[]{:S(2)}) %collective-permute-start.31) | collective-permute-done | bytes 73760 | tf_op jit(solution)/shard_map/ppermute | solution.py:23
  118.4 5.6 %spread.1 = (f32[32,128,128]{2,1,0:T(8,128)S(1)}, bf16[32,128,128]{2,1,0:T(8,128)(2,1)}) custom-call(s32[64]{0:T(128)S(1)} %and_add_fusion.idx, s32[64]{0:T(128)S(1)} %copy-done.10, bf16[64,128,128]{2,1,0:T(8,128)(2,1)S(1)} %copy-done, bf16[2,128,128]{2,1,0:T(8,128)(2,1)S(1)} %bitcast.82), custom_call_target="tpu_custom_call" | custom-call | flops 268435456 | bytes 6291456 | tf_op jit(solution)/shard_map/spread/pallas_call | solution.py:167
  123.9 1.3 copy-done.1
  125.3 1.5 collective-permute-start.21
  126.8 2.9 %collective-permute-start.33 = (bf16[32,1152]{1,0:T(8,128)(2,1)S(1)}, bf16[32,1152]{1,0:T(8,128)(2,1)S(1)}, u32[]{:S(2)}, u32[]{:S(2)}) collective-permute-start(bf16[32,1152]{1,0:T(8,128)(2,1)S(1)} %get-tuple-element.21), channel_id=1, source_target_pairs={{0,112},{8,120},{16,0},{24,8},{32,16},{40,24},{48,32},{56,40},{64,... | collective-permute-start | bytes 221192 | tf_op jit(solution)/shard_map/ppermute | solution.py:23
  129.7 1.7 collective-permute-done.33
  131.4 3.4 %collective-permute-start.35 = (bf16[32,1152]{1,0:T(8,128)(2,1)S(1)}, bf16[32,1152]{1,0:T(8,128)(2,1)S(1)}, u32[]{:S(2)}, u32[]{:S(2)}) collective-permute-start(bf16[32,1152]{1,0:T(8,128)(2,1)S(1)} %collective-permute-done.33), channel_id=1, source_target_pairs={{0,112},{8,120},{16,0},{24,8},{32,16},{40,24},{48,32},{56,40},{64,... | collective-permute-start | bytes 221192 | tf_op jit(solution)/shard_map/ppermute | solution.py:23
  136.2 3.0 %collective-permute-start.37 = (bf16[32,1152]{1,0:T(8,128)(2,1)S(1)}, bf16[32,1152]{1,0:T(8,128)(2,1)S(1)}, u32[]{:S(2)}, u32[]{:S(2)}) collective-permute-start(bf16[32,1152]{1,0:T(8,128)(2,1)S(1)} %collective-permute-done.35), channel_id=1, source_target_pairs={{0,112},{8,120},{16,0},{24,8},{32,16},{40,24},{48,32},{56,40},{64,... | collective-permute-start | bytes 221192 | tf_op jit(solution)/shard_map/ppermute | solution.py:23
  139.4 1.3 collective-permute-done.37
  140.7 3.1 %collective-permute-done.38 = bf16[32,1152]{1,0:T(8,128)(2,1)S(1)} collective-permute-done((bf16[32,1152]{1,0:T(8,128)(2,1)S(1)}, bf16[32,1152]{1,0:T(8,128)(2,1)S(1)}, u32[]{:S(2)}, u32[]{:S(2)}) %collective-permute-start.38) | collective-permute-done | bytes 73760 | tf_op jit(solution)/shard_map/ppermute | solution.py:23
  144.6 2.8 %collective-permute-done.39 = bf16[32,1152]{1,0:T(8,128)(2,1)S(1)} collective-permute-done((bf16[32,1152]{1,0:T(8,128)(2,1)S(1)}, bf16[32,1152]{1,0:T(8,128)(2,1)S(1)}, u32[]{:S(2)}, u32[]{:S(2)}) %collective-permute-start.39) | collective-permute-done | bytes 73760 | tf_op jit(solution)/shard_map/ppermute | solution.py:23
  148.2 4.5 %collective-permute-start.40 = (bf16[64,1152]{1,0:T(8,128)(2,1)}, bf16[64,1152]{1,0:T(8,128)(2,1)}, u32[]{:S(2)}, u32[]{:S(2)}) collective-permute-start(bf16[64,1152]{1,0:T(8,128)(2,1)} %pad_maximum_fusion), channel_id=1, source_target_pairs={{0,8},{8,0},{16,24},{24,16},{32,40},{40,32},{48,56},{56,48},{64,72... | collective-permute-start | bytes 442376 | tf_op jit(solution)/shard_map/ppermute | solution.py:23
  152.7 1.5 convert_add_fusion
  154.2 1.3 copy-done.11
  157.1 12.2 %collective-permute-done.22 = bf16[8,256,128]{2,1,0:T(8,128)(2,1)S(1)} collective-permute-done((bf16[8,256,128]{2,1,0:T(8,128)(2,1)S(1)}, bf16[8,256,128]{2,1,0:T(8,128)(2,1)S(1)}, u32[]{:S(2)}, u32[]{:S(2)}) %collective-permute-start.22) | collective-permute-done | bytes 524320 | tf_op jit(solution)/shard_map/ppermute | solution.py:23
  169.2 1.4 fusion.12
  170.7 4.1 %collective-permute-start.23 = (bf16[256,128]{1,0:T(8,128)(2,1)S(1)}, bf16[256,128]{1,0:T(8,128)(2,1)S(1)}, u32[]{:S(2)}, u32[]{:S(2)}) collective-permute-start(bf16[256,128]{1,0:T(8,128)(2,1)S(1)} %get-tuple-element.24), channel_id=1, source_target_pairs={{0,64},{8,72},{16,80},{24,88},{32,96},{40,104},{48,112},{56,120},{... | collective-permute-start | bytes 196616 | tf_op jit(solution)/shard_map/ppermute | solution.py:23
  175.7 4.5 %collective-permute-start.25 = (bf16[256,128]{1,0:T(8,128)(2,1)S(1)}, bf16[256,128]{1,0:T(8,128)(2,1)S(1)}, u32[]{:S(2)}, u32[]{:S(2)}) collective-permute-start(bf16[256,128]{1,0:T(8,128)(2,1)S(1)} %get-tuple-element.29), channel_id=1, source_target_pairs={{0,80},{8,88},{16,96},{24,104},{32,112},{40,120},{48,0},{56,8},{64... | collective-permute-start | bytes 196616 | tf_op jit(solution)/shard_map/ppermute | solution.py:23
  180.2 3.6 %collective-permute-start.27 = (bf16[256,128]{1,0:T(8,128)(2,1)S(1)}, bf16[256,128]{1,0:T(8,128)(2,1)S(1)}, u32[]{:S(2)}, u32[]{:S(2)}) collective-permute-start(bf16[256,128]{1,0:T(8,128)(2,1)S(1)} %get-tuple-element.27), channel_id=1, source_target_pairs={{0,96},{8,104},{16,112},{24,120},{32,0},{40,8},{48,16},{56,24},{64... | collective-permute-start | bytes 196616 | tf_op jit(solution)/shard_map/ppermute | solution.py:23
  183.8 2.7 %collective-permute-start.29 = (bf16[256,128]{1,0:T(8,128)(2,1)S(1)}, bf16[256,128]{1,0:T(8,128)(2,1)S(1)}, u32[]{:S(2)}, u32[]{:S(2)}) collective-permute-start(bf16[256,128]{1,0:T(8,128)(2,1)S(1)} %get-tuple-element.25), channel_id=1, source_target_pairs={{0,112},{8,120},{16,0},{24,8},{32,16},{40,24},{48,32},{56,40},{64,... | collective-permute-start | bytes 196616 | tf_op jit(solution)/shard_map/ppermute | solution.py:23
  187.0 1.8 collective-permute-done.28
  (114 shorter events, 29.1 us)
Async XLA Ops:
  0.6 68.2 %copy-start = (bf16[64,128,128]{2,1,0:T(8,128)(2,1)S(1)}, bf16[64,128,128]{2,1,0:T(8,128)(2,1)}, u32[]{:S(2)}) copy-start(bf16[64,128,128]{2,1,0:T(8,128)(2,1)} %tiles.3) | copy-start | bytes 6291460
  0.6 68.2 %copy-start.10 = (s32[64]{0:T(128)S(1)}, s32[64]{0:T(128)}, u32[]{:S(2)}) copy-start(s32[64]{0:T(128)} %dest.3) | copy-start | bytes 772
  0.7 6.0 %collective-permute-start = (bf16[256,128]{1,0:T(8,128)(2,1)}, bf16[256,128]{1,0:T(8,128)(2,1)S(1)}, u32[]{:S(2)}, u32[]{:S(2)}) collective-permute-start(bf16[256,128]{1,0:T(8,128)(2,1)} %param.8), channel_id=1, source_target_pairs={{0,128},{8,136},{16,144},{24,152},{32,160},{40,168},{48,176},{56,1... | collective-permute-start | bytes 196616 | tf_op jit(solution)/shard_map/ppermute | solution.py:23
  5.1 31.2 %copy-start.14 = (bf16[128]{0:T(256)(128)(2,1)S(1)}, bf16[128]{0:T(256)(128)(2,1)}, u32[]{:S(2)}) copy-start(bf16[128]{0:T(256)(128)(2,1)} %param.10) | copy-start | bytes 772
  7.3 8.7 %collective-permute-start.4 = (bf16[512,128]{1,0:T(8,128)(2,1)}, bf16[512,128]{1,0:T(8,128)(2,1)S(1)}, u32[]{:S(2)}, u32[]{:S(2)}) collective-permute-start(bf16[512,128]{1,0:T(8,128)(2,1)} %get-tuple-element.39), channel_id=1, source_target_pairs={{0,16},{8,24},{16,32},{24,40},{32,48},{40,56},{48,64},{56,72},{64,... | collective-permute-start | bytes 393224 | tf_op jit(solution)/shard_map/ppermute | solution.py:23
  10.4 6.4 %collective-permute-start.1 = (bf16[512,128]{1,0:T(8,128)(2,1)}, bf16[512,128]{1,0:T(8,128)(2,1)S(1)}, u32[]{:S(2)}, u32[]{:S(2)}) collective-permute-start(bf16[512,128]{1,0:T(8,128)(2,1)} %get-tuple-element.39), channel_id=1, source_target_pairs={{0,112},{8,120},{16,0},{24,8},{32,16},{40,24},{48,32},{56,40},{64,... | collective-permute-start | bytes 393224 | tf_op jit(solution)/shard_map/ppermute | solution.py:23
  16.0 5.0 %collective-permute-start.5 = (bf16[512,128]{1,0:T(8,128)(2,1)S(1)}, bf16[512,128]{1,0:T(8,128)(2,1)S(1)}, u32[]{:S(2)}, u32[]{:S(2)}) collective-permute-start(bf16[512,128]{1,0:T(8,128)(2,1)S(1)} %collective-permute-done.4), channel_id=1, source_target_pairs={{0,16},{8,24},{16,32},{24,40},{32,48},{40,56},{48,64},{56,72},{64,... | collective-permute-start | bytes 393224 | tf_op jit(solution)/shard_map/ppermute | solution.py:23
  16.8 5.7 %collective-permute-start.2 = (bf16[512,128]{1,0:T(8,128)(2,1)S(1)}, bf16[512,128]{1,0:T(8,128)(2,1)S(1)}, u32[]{:S(2)}, u32[]{:S(2)}) collective-permute-start(bf16[512,128]{1,0:T(8,128)(2,1)S(1)} %collective-permute-done.1), channel_id=1, source_target_pairs={{0,112},{8,120},{16,0},{24,8},{32,16},{40,24},{48,32},{56,40},{64,... | collective-permute-start | bytes 393224 | tf_op jit(solution)/shard_map/ppermute | solution.py:23
  21.1 5.0 %collective-permute-start.6 = (bf16[512,128]{1,0:T(8,128)(2,1)S(1)}, bf16[512,128]{1,0:T(8,128)(2,1)S(1)}, u32[]{:S(2)}, u32[]{:S(2)}) collective-permute-start(bf16[512,128]{1,0:T(8,128)(2,1)S(1)} %collective-permute-done.5), channel_id=1, source_target_pairs={{0,16},{8,24},{16,32},{24,40},{32,48},{40,56},{48,64},{56,72},{64,... | collective-permute-start | bytes 393224 | tf_op jit(solution)/shard_map/ppermute | solution.py:23
  22.5 4.6 %collective-permute-start.3 = (bf16[512,128]{1,0:T(8,128)(2,1)S(1)}, bf16[512,128]{1,0:T(8,128)(2,1)S(1)}, u32[]{:S(2)}, u32[]{:S(2)}) collective-permute-start(bf16[512,128]{1,0:T(8,128)(2,1)S(1)} %collective-permute-done.2), channel_id=1, source_target_pairs={{0,112},{8,120},{16,0},{24,8},{32,16},{40,24},{48,32},{56,40},{64,... | collective-permute-start | bytes 393224 | tf_op jit(solution)/shard_map/ppermute | solution.py:23
  26.1 5.0 %collective-permute-start.7 = (bf16[512,128]{1,0:T(8,128)(2,1)S(1)}, bf16[512,128]{1,0:T(8,128)(2,1)S(1)}, u32[]{:S(2)}, u32[]{:S(2)}) collective-permute-start(bf16[512,128]{1,0:T(8,128)(2,1)S(1)} %collective-permute-done.6), channel_id=1, source_target_pairs={{0,16},{8,24},{16,32},{24,40},{32,48},{40,56},{48,64},{56,72},{64,... | collective-permute-start | bytes 393224 | tf_op jit(solution)/shard_map/ppermute | solution.py:23
  31.2 37.6 %collective-permute-start.8 = (bf16[4096,128]{1,0:T(8,128)(2,1)S(1)}, bf16[4096,128]{1,0:T(8,128)(2,1)}, u32[]{:S(2)}, u32[]{:S(2)}) collective-permute-start(bf16[4096,128]{1,0:T(8,128)(2,1)S(1)} %constant_dynamic-update-slice_fusion.2), channel_id=1, source_target_pairs={{0,8},{8,0},{16,24},{24,16},{32,40},{40,32},{48,56},{56,48},{64,72... | collective-permute-start | bytes 3145736 | tf_op jit(solution)/shard_map/ppermute | solution.py:23
  36.9 8.3 %collective-permute-start.13 = (bf16[784,128]{1,0:T(8,128)(2,1)}, bf16[784,128]{1,0:T(8,128)(2,1)S(1)}, u32[]{:S(2)}, u32[]{:S(2)}) collective-permute-start(bf16[784,128]{1,0:T(8,128)(2,1)} %get-tuple-element.51), channel_id=1, source_target_pairs={{0,4},{1,5},{2,6},{3,7},{4,0},{5,1},{6,2},{7,3},{8,12},{9,13},{10,... | collective-permute-start | bytes 602120 | tf_op jit(solution)/shard_map/ppermute | solution.py:27
  45.2 11.5 %collective-permute-start.14 = (bf16[1568,128]{1,0:T(8,128)(2,1)S(1)}, bf16[1568,128]{1,0:T(8,128)(2,1)}, u32[]{:S(2)}, u32[]{:S(2)}) collective-permute-start(bf16[1568,128]{1,0:T(8,128)(2,1)S(1)} %constant_dynamic-update-slice_fusion.17.refs_0_), channel_id=1, source_target_pairs={{0,1},{1,2},{2,3},{3,0},{4,5},{5,6},{6,7},{7,4},{8,9},{9,10},{10,1... | collective-permute-start | bytes 1204232 | tf_op jit(solution)/shard_map/ppermute | solution.py:27
  46.6 11.9 %collective-permute-start.15 = (bf16[1568,128]{1,0:T(8,128)(2,1)S(1)}, bf16[1568,128]{1,0:T(8,128)(2,1)}, u32[]{:S(2)}, u32[]{:S(2)}) collective-permute-start(bf16[1568,128]{1,0:T(8,128)(2,1)S(1)} %constant_dynamic-update-slice_fusion.17.refs_0_), channel_id=1, source_target_pairs={{0,3},{1,0},{2,1},{3,2},{4,7},{5,4},{6,5},{7,6},{8,11},{9,8},{10,9... | collective-permute-start | bytes 1204232 | tf_op jit(solution)/shard_map/ppermute | solution.py:27
  48.1 18.3 %collective-permute-start.16 = (bf16[1568,128]{1,0:T(8,128)(2,1)S(1)}, bf16[1568,128]{1,0:T(8,128)(2,1)}, u32[]{:S(2)}, u32[]{:S(2)}) collective-permute-start(bf16[1568,128]{1,0:T(8,128)(2,1)S(1)} %constant_dynamic-update-slice_fusion.17.refs_0_), channel_id=1, source_target_pairs={{0,2},{1,3},{2,0},{3,1},{4,6},{5,7},{6,4},{7,5},{8,10},{9,11},{10,... | collective-permute-start | bytes 1204232 | tf_op jit(solution)/shard_map/ppermute | solution.py:27
  49.7 30.8 %collective-permute-start.17 = (bf16[1568,128]{1,0:T(8,128)(2,1)S(1)}, bf16[1568,128]{1,0:T(8,128)(2,1)S(1)}, u32[]{:S(2)}, u32[]{:S(2)}) collective-permute-start(bf16[1568,128]{1,0:T(8,128)(2,1)S(1)} %constant_dynamic-update-slice_fusion.17.refs_0_), channel_id=1, source_target_pairs={{0,8},{8,0},{16,24},{24,16},{32,40},{40,32},{48,56},{56,48},{64,72... | collective-permute-start | bytes 1204232 | tf_op jit(solution)/shard_map/ppermute | solution.py:23
  56.8 26.3 %collective-permute-start.18 = (bf16[1568,128]{1,0:T(8,128)(2,1)}, bf16[1568,128]{1,0:T(8,128)(2,1)S(1)}, u32[]{:S(2)}, u32[]{:S(2)}) collective-permute-start(bf16[1568,128]{1,0:T(8,128)(2,1)} %collective-permute-done.14.refs_1_), channel_id=1, source_target_pairs={{0,8},{8,0},{16,24},{24,16},{32,40},{40,32},{48,56},{56,48},{64,72... | collective-permute-start | bytes 1204232 | tf_op jit(solution)/shard_map/ppermute | solution.py:23
  58.5 25.4 %collective-permute-start.19 = (bf16[1568,128]{1,0:T(8,128)(2,1)}, bf16[1568,128]{1,0:T(8,128)(2,1)}, u32[]{:S(2)}, u32[]{:S(2)}) collective-permute-start(bf16[1568,128]{1,0:T(8,128)(2,1)} %collective-permute-done.15.refs_2_), channel_id=1, source_target_pairs={{0,8},{8,0},{16,24},{24,16},{32,40},{40,32},{48,56},{56,48},{64,72... | collective-permute-start | bytes 1204232 | tf_op jit(solution)/shard_map/ppermute | solution.py:23
  66.5 17.4 %collective-permute-start.20 = (bf16[1568,128]{1,0:T(8,128)(2,1)}, bf16[1568,128]{1,0:T(8,128)(2,1)}, u32[]{:S(2)}, u32[]{:S(2)}) collective-permute-start(bf16[1568,128]{1,0:T(8,128)(2,1)} %collective-permute-done.16.refs_3_), channel_id=1, source_target_pairs={{0,8},{8,0},{16,24},{24,16},{32,40},{40,32},{48,56},{56,48},{64,72... | collective-permute-start | bytes 1204232 | tf_op jit(solution)/shard_map/ppermute | solution.py:23
  74.0 15.2 %copy-start.3 = (bf16[128,1024]{1,0:T(8,128)(2,1)S(1)}, bf16[128,1024]{1,0:T(8,128)(2,1)}, u32[]{:S(2)}) copy-start(bf16[128,1024]{1,0:T(8,128)(2,1)} %w_own.1) | copy-start | bytes 786436
  74.0 5.5 %collective-permute-start.9 = (bf16[256,128]{1,0:T(8,128)(2,1)S(1)}, bf16[256,128]{1,0:T(8,128)(2,1)S(1)}, u32[]{:S(2)}, u32[]{:S(2)}) collective-permute-start(bf16[256,128]{1,0:T(8,128)(2,1)S(1)} %aggregate.1), channel_id=1, source_target_pairs={{0,4},{1,5},{2,6},{3,7},{4,0},{5,1},{6,2},{7,3},{8,12},{9,13},{10,... | collective-permute-start | bytes 196616 | tf_op jit(solution)/shard_map/ppermute | solution.py:27
  79.5 8.6 %collective-permute-start.10 = (bf16[512,128]{1,0:T(8,128)(2,1)S(1)}, bf16[512,128]{1,0:T(8,128)(2,1)S(1)}, u32[]{:S(2)}, u32[]{:S(2)}) collective-permute-start(bf16[512,128]{1,0:T(8,128)(2,1)S(1)} %pad_maximum_fusion.1.p0), channel_id=1, source_target_pairs={{0,1},{1,2},{2,3},{3,0},{4,5},{5,6},{6,7},{7,4},{8,9},{9,10},{10,1... | collective-permute-start | bytes 393224 | tf_op jit(solution)/shard_map/ppermute | solution.py:27
  81.2 7.5 %collective-permute-start.11 = (bf16[512,128]{1,0:T(8,128)(2,1)S(1)}, bf16[512,128]{1,0:T(8,128)(2,1)}, u32[]{:S(2)}, u32[]{:S(2)}) collective-permute-start(bf16[512,128]{1,0:T(8,128)(2,1)S(1)} %pad_maximum_fusion.1.p0), channel_id=1, source_target_pairs={{0,3},{1,0},{2,1},{3,2},{4,7},{5,4},{6,5},{7,6},{8,11},{9,8},{10,9... | collective-permute-start | bytes 393224 | tf_op jit(solution)/shard_map/ppermute | solution.py:27
  83.8 5.4 %collective-permute-start.12 = (bf16[512,128]{1,0:T(8,128)(2,1)S(1)}, bf16[512,128]{1,0:T(8,128)(2,1)}, u32[]{:S(2)}, u32[]{:S(2)}) collective-permute-start(bf16[512,128]{1,0:T(8,128)(2,1)S(1)} %pad_maximum_fusion.1.p0), channel_id=1, source_target_pairs={{0,2},{1,3},{2,0},{3,1},{4,6},{5,7},{6,4},{7,5},{8,10},{9,11},{10,... | collective-permute-start | bytes 393224 | tf_op jit(solution)/shard_map/ppermute | solution.py:27
  90.2 12.4 %copy-start.12 = (s32[8]{0:T(128)S(1)}, s32[8]{0:T(128)}, u32[]{:S(2)}) copy-start(s32[8]{0:T(128)} %constant.66.clone) | copy-start | bytes 100
  92.8 3.8 %collective-permute-start.30 = (f32[64,1152]{1,0:T(8,128)S(1)}, f32[64,1152]{1,0:T(8,128)S(1)}, u32[]{:S(2)}, u32[]{:S(2)}) collective-permute-start(f32[64,1152]{1,0:T(8,128)S(1)} %constant_dynamic-slice_fusion), channel_id=1, source_target_pairs={{0,8},{8,0},{16,24},{24,16},{32,40},{40,32},{48,56},{56,48},{64,72... | collective-permute-start | bytes 884744 | tf_op jit(solution)/shard_map/ppermute | solution.py:23
  98.3 3.3 %collective-permute-start.31 = (bf16[32,1152]{1,0:T(8,128)(2,1)S(1)}, bf16[32,1152]{1,0:T(8,128)(2,1)S(1)}, u32[]{:S(2)}, u32[]{:S(2)}) collective-permute-start(bf16[32,1152]{1,0:T(8,128)(2,1)S(1)} %dynamic-slice_convert_fusion), channel_id=1, source_target_pairs={{0,128},{8,136},{16,144},{24,152},{32,160},{40,168},{48,176},{56,1... | collective-permute-start | bytes 221192 | tf_op jit(solution)/shard_map/ppermute | solution.py:23
  102.5 27.2 %collective-permute-start.32 = (bf16[32,1152]{1,0:T(8,128)(2,1)S(1)}, bf16[32,1152]{1,0:T(8,128)(2,1)S(1)}, u32[]{:S(2)}, u32[]{:S(2)}) collective-permute-start(bf16[32,1152]{1,0:T(8,128)(2,1)S(1)} %get-tuple-element.21), channel_id=1, source_target_pairs={{0,16},{8,24},{16,32},{24,40},{32,48},{40,56},{48,64},{56,72},{64,... | collective-permute-start | bytes 221192 | tf_op jit(solution)/shard_map/ppermute | solution.py:23
  125.3 27.4 %copy-start.2 = (f32[32,128,128]{2,1,0:T(8,128)S(1)}, f32[32,128,128]{2,1,0:T(8,128)}, u32[]{:S(2)}) copy-start(f32[32,128,128]{2,1,0:T(8,128)} %copy-done.1) | copy-start | bytes 6291460
  125.3 27.4 %collective-permute-start.21 = (bf16[32,128,128]{2,1,0:T(8,128)(2,1)}, bf16[32,128,128]{2,1,0:T(8,128)(2,1)}, u32[]{:S(2)}, u32[]{:S(2)}) collective-permute-start(bf16[32,128,128]{2,1,0:T(8,128)(2,1)} %get-tuple-element.18), channel_id=1, source_target_pairs={{0,8},{8,0},{16,24},{24,16},{32,40},{40,32},{48,56},{56,48},{64,72... | collective-permute-start | bytes 3145736 | tf_op jit(solution)/shard_map/ppermute | solution.py:23
  126.8 4.6 %collective-permute-start.33 = (bf16[32,1152]{1,0:T(8,128)(2,1)S(1)}, bf16[32,1152]{1,0:T(8,128)(2,1)S(1)}, u32[]{:S(2)}, u32[]{:S(2)}) collective-permute-start(bf16[32,1152]{1,0:T(8,128)(2,1)S(1)} %get-tuple-element.21), channel_id=1, source_target_pairs={{0,112},{8,120},{16,0},{24,8},{32,16},{40,24},{48,32},{56,40},{64,... | collective-permute-start | bytes 221192 | tf_op jit(solution)/shard_map/ppermute | solution.py:23
  129.7 5.1 %collective-permute-start.34 = (bf16[32,1152]{1,0:T(8,128)(2,1)S(1)}, bf16[32,1152]{1,0:T(8,128)(2,1)S(1)}, u32[]{:S(2)}, u32[]{:S(2)}) collective-permute-start(bf16[32,1152]{1,0:T(8,128)(2,1)S(1)} %collective-permute-done.32), channel_id=1, source_target_pairs={{0,16},{8,24},{16,32},{24,40},{32,48},{40,56},{48,64},{56,72},{64,... | collective-permute-start | bytes 221192 | tf_op jit(solution)/shard_map/ppermute | solution.py:23
  131.4 4.8 %collective-permute-start.35 = (bf16[32,1152]{1,0:T(8,128)(2,1)S(1)}, bf16[32,1152]{1,0:T(8,128)(2,1)S(1)}, u32[]{:S(2)}, u32[]{:S(2)}) collective-permute-start(bf16[32,1152]{1,0:T(8,128)(2,1)S(1)} %collective-permute-done.33), channel_id=1, source_target_pairs={{0,112},{8,120},{16,0},{24,8},{32,16},{40,24},{48,32},{56,40},{64,... | collective-permute-start | bytes 221192 | tf_op jit(solution)/shard_map/ppermute | solution.py:23
  134.8 4.5 %collective-permute-start.36 = (bf16[32,1152]{1,0:T(8,128)(2,1)S(1)}, bf16[32,1152]{1,0:T(8,128)(2,1)S(1)}, u32[]{:S(2)}, u32[]{:S(2)}) collective-permute-start(bf16[32,1152]{1,0:T(8,128)(2,1)S(1)} %collective-permute-done.34), channel_id=1, source_target_pairs={{0,16},{8,24},{16,32},{24,40},{32,48},{40,56},{48,64},{56,72},{64,... | collective-permute-start | bytes 221192 | tf_op jit(solution)/shard_map/ppermute | solution.py:23
  136.2 4.4 %collective-permute-start.37 = (bf16[32,1152]{1,0:T(8,128)(2,1)S(1)}, bf16[32,1152]{1,0:T(8,128)(2,1)S(1)}, u32[]{:S(2)}, u32[]{:S(2)}) collective-permute-start(bf16[32,1152]{1,0:T(8,128)(2,1)S(1)} %collective-permute-done.35), channel_id=1, source_target_pairs={{0,112},{8,120},{16,0},{24,8},{32,16},{40,24},{48,32},{56,40},{64,... | collective-permute-start | bytes 221192 | tf_op jit(solution)/shard_map/ppermute | solution.py:23
  139.3 4.4 %collective-permute-start.38 = (bf16[32,1152]{1,0:T(8,128)(2,1)S(1)}, bf16[32,1152]{1,0:T(8,128)(2,1)S(1)}, u32[]{:S(2)}, u32[]{:S(2)}) collective-permute-start(bf16[32,1152]{1,0:T(8,128)(2,1)S(1)} %collective-permute-done.36), channel_id=1, source_target_pairs={{0,16},{8,24},{16,32},{24,40},{32,48},{40,56},{48,64},{56,72},{64,... | collective-permute-start | bytes 221192 | tf_op jit(solution)/shard_map/ppermute | solution.py:23
  143.9 3.5 %collective-permute-start.39 = (bf16[32,1152]{1,0:T(8,128)(2,1)S(1)}, bf16[32,1152]{1,0:T(8,128)(2,1)S(1)}, u32[]{:S(2)}, u32[]{:S(2)}) collective-permute-start(bf16[32,1152]{1,0:T(8,128)(2,1)S(1)} %fusion.9), channel_id=1, source_target_pairs={{0,128},{8,136},{16,144},{24,152},{32,160},{40,168},{48,176},{56,1... | collective-permute-start | bytes 221192 | tf_op jit(solution)/shard_map/ppermute | solution.py:23
  148.2 7.9 %collective-permute-start.40 = (bf16[64,1152]{1,0:T(8,128)(2,1)}, bf16[64,1152]{1,0:T(8,128)(2,1)}, u32[]{:S(2)}, u32[]{:S(2)}) collective-permute-start(bf16[64,1152]{1,0:T(8,128)(2,1)} %pad_maximum_fusion), channel_id=1, source_target_pairs={{0,8},{8,0},{16,24},{24,16},{32,40},{40,32},{48,56},{56,48},{64,72... | collective-permute-start | bytes 442376 | tf_op jit(solution)/shard_map/ppermute | solution.py:23
  154.2 1.3 copy-start.11
  155.6 13.6 %collective-permute-start.22 = (bf16[8,256,128]{2,1,0:T(8,128)(2,1)S(1)}, bf16[8,256,128]{2,1,0:T(8,128)(2,1)S(1)}, u32[]{:S(2)}, u32[]{:S(2)}) collective-permute-start(bf16[8,256,128]{2,1,0:T(8,128)(2,1)S(1)} %fusion.1), channel_id=1, source_target_pairs={{0,128},{8,136},{16,144},{24,152},{32,160},{40,168},{48,176},{56,1... | collective-permute-start | bytes 1572872 | tf_op jit(solution)/shard_map/ppermute | solution.py:23
  170.7 13.1 %collective-permute-start.23 = (bf16[256,128]{1,0:T(8,128)(2,1)S(1)}, bf16[256,128]{1,0:T(8,128)(2,1)S(1)}, u32[]{:S(2)}, u32[]{:S(2)}) collective-permute-start(bf16[256,128]{1,0:T(8,128)(2,1)S(1)} %get-tuple-element.24), channel_id=1, source_target_pairs={{0,64},{8,72},{16,80},{24,88},{32,96},{40,104},{48,112},{56,120},{... | collective-permute-start | bytes 196616 | tf_op jit(solution)/shard_map/ppermute | solution.py:23
  174.8 8.9 %collective-permute-start.24 = (bf16[256,128]{1,0:T(8,128)(2,1)S(1)}, bf16[256,128]{1,0:T(8,128)(2,1)S(1)}, u32[]{:S(2)}, u32[]{:S(2)}) collective-permute-start(bf16[256,128]{1,0:T(8,128)(2,1)S(1)} %get-tuple-element.30), channel_id=1, source_target_pairs={{0,48},{8,56},{16,64},{24,72},{32,80},{40,88},{48,96},{56,104},{64... | collective-permute-start | bytes 196616 | tf_op jit(solution)/shard_map/ppermute | solution.py:23
  175.7 11.2 %collective-permute-start.25 = (bf16[256,128]{1,0:T(8,128)(2,1)S(1)}, bf16[256,128]{1,0:T(8,128)(2,1)S(1)}, u32[]{:S(2)}, u32[]{:S(2)}) collective-permute-start(bf16[256,128]{1,0:T(8,128)(2,1)S(1)} %get-tuple-element.29), channel_id=1, source_target_pairs={{0,80},{8,88},{16,96},{24,104},{32,112},{40,120},{48,0},{56,8},{64... | collective-permute-start | bytes 196616 | tf_op jit(solution)/shard_map/ppermute | solution.py:23
  180.2 6.8 %collective-permute-start.26 = (bf16[256,128]{1,0:T(8,128)(2,1)S(1)}, bf16[256,128]{1,0:T(8,128)(2,1)S(1)}, u32[]{:S(2)}, u32[]{:S(2)}) collective-permute-start(bf16[256,128]{1,0:T(8,128)(2,1)S(1)} %get-tuple-element.28), channel_id=1, source_target_pairs={{0,32},{8,40},{16,48},{24,56},{32,64},{40,72},{48,80},{56,88},{64,... | collective-permute-start | bytes 196616 | tf_op jit(solution)/shard_map/ppermute | solution.py:23
  180.2 6.8 %collective-permute-start.27 = (bf16[256,128]{1,0:T(8,128)(2,1)S(1)}, bf16[256,128]{1,0:T(8,128)(2,1)S(1)}, u32[]{:S(2)}, u32[]{:S(2)}) collective-permute-start(bf16[256,128]{1,0:T(8,128)(2,1)S(1)} %get-tuple-element.27), channel_id=1, source_target_pairs={{0,96},{8,104},{16,112},{24,120},{32,0},{40,8},{48,16},{56,24},{64... | collective-permute-start | bytes 196616 | tf_op jit(solution)/shard_map/ppermute | solution.py:23
  183.8 5.0 %collective-permute-start.28 = (bf16[256,128]{1,0:T(8,128)(2,1)S(1)}, bf16[256,128]{1,0:T(8,128)(2,1)S(1)}, u32[]{:S(2)}, u32[]{:S(2)}) collective-permute-start(bf16[256,128]{1,0:T(8,128)(2,1)S(1)} %get-tuple-element.26), channel_id=1, source_target_pairs={{0,16},{8,24},{16,32},{24,40},{32,48},{40,56},{48,64},{56,72},{64,... | collective-permute-start | bytes 196616 | tf_op jit(solution)/shard_map/ppermute | solution.py:23
  183.8 5.0 %collective-permute-start.29 = (bf16[256,128]{1,0:T(8,128)(2,1)S(1)}, bf16[256,128]{1,0:T(8,128)(2,1)S(1)}, u32[]{:S(2)}, u32[]{:S(2)}) collective-permute-start(bf16[256,128]{1,0:T(8,128)(2,1)S(1)} %get-tuple-element.25), channel_id=1, source_target_pairs={{0,112},{8,120},{16,0},{24,8},{32,16},{40,24},{48,32},{56,40},{64,... | collective-permute-start | bytes 196616 | tf_op jit(solution)/shard_map/ppermute | solution.py:23
  (8 other events, 7.1 us)

commit v2 on v1

v2 whole, which is shorter than its diff:
```python
import functools

import jax
import jax.numpy as jnp
from jax import lax
from jax.experimental import pallas as pl
from jax.experimental.pallas import tpu as pltpu
from jax.sharding import PartitionSpec as P

bf16 = jnp.bfloat16
f32 = jnp.float32
B = 128
NZ = 8
VM = pl.BlockSpec(memory_space=pltpu.VMEM)
SM = pl.BlockSpec(memory_space=pltpu.SMEM)


def row_send(v, dx=0, dz=0, dc=0):
    perm = []
    for i in range(32):
        x, z, c = i >> 4, (i >> 1) & 7, i & 1
        perm.append((i, ((x ^ dx) << 4) | (((z + dz) % NZ) << 1) | (c ^ dc)))
    return lax.ppermute(v, "row", perm)


def feat_send(v, dx=0, dy=0):
    return lax.ppermute(v, "feat", [(i, (((i >> 2) ^ dx) << 2) | ((i + dy) & 3)) for i in range(8)])


def params(mib=20):
    return pltpu.CompilerParams(vmem_limit_bytes=mib << 20)


def spin_send(v, k):
    perm = []
    for i in range(32):
        x, z, c = i >> 4, (i >> 1) & 7, i & 1
        perm.append((i, (x << 4) | (((z + (k if c == 0 else -k)) % NZ) << 1) | c))
    return lax.ppermute(v, "row", perm)


def after(v, *deps):
    return lax.optimization_barrier((v, *deps))[0]


def cost(flops, nbytes):
    return pl.CostEstimate(flops=flops, bytes_accessed=nbytes, transcendentals=0)


def agg_body(ids, idx, dest, tiles, *refs):
    near, far, out, src = refs[0:10], refs[10:19], refs[19], refs[20]
    core = ids[0] & 1

    def put(dc, dz, dx, v):
        src[pl.ds(((dc * NZ + dz) * 2 + dx) * 2, 2)] = v

    both, x0, o4, o1, o2, o3, p4, p1, p2, p3 = near
    put(0, 0, 0, both[0:2])
    put(1, 0, 0, both[2:4])
    put(0, 0, 1, x0[...])
    put(0, 4, 0, o4[...])
    put(0, 4, 1, p4[...])
    put(1, 0, 1, far[0][...])
    put(1, 4, 0, far[1][...])
    put(1, 4, 1, far[5][...])
    for k in (1, 2, 3):
        mine = jnp.where(core == 0, NZ - k, k)
        theirs = NZ - mine
        for dx, (n, f) in enumerate((((o1, o2, o3), far[2:5]), ((p1, p2, p3), far[6:9]))):
            put(0, mine, dx, n[k - 1][0:2])
            put(1, mine, dx, n[k - 1][2:4])
            put(1, theirs, dx, f[k - 1][0:2])
            put(0, theirs, dx, f[k - 1][2:4])
    group = 4

    def step(g, acc):
        lhs, rhs = [], []
        for u in range(group):
            t = g * group + u
            a = tiles[t]
            zero = jnp.zeros_like(a)
            d = dest[t]
            lhs.append(jnp.concatenate([jnp.where(d == 0, a, zero), jnp.where(d == 1, a, zero)], axis=0))
            rhs.append(src[idx[t]])
        return acc + jnp.dot(
            jnp.concatenate(lhs, axis=1), jnp.concatenate(rhs, axis=0), preferred_element_type=f32
        )

    acc = lax.fori_loop(0, 64 // group, step, jnp.zeros((2 * B, B), f32))
    out[...] = acc.astype(bf16)


def aggregate(ids, idx, dest, tiles, near, far):
    parts = [v.reshape(-1, B, B) for v in (*near, *far)]
    return pl.pallas_call(
        agg_body,
        out_shape=jax.ShapeDtypeStruct((2 * B, B), bf16),
        in_specs=[SM, SM, SM] + [VM] * 20,
        out_specs=VM,
        scratch_shapes=[pltpu.VMEM((64, B, B), bf16)],
        compiler_params=params(),
        cost_estimate=cost(2 * 64 * B**3, 4 << 20),
        name="aggregate",
    )(ids, idx, dest, tiles, *parts)


def lay_body(ids, *refs):
    own, other = refs[0:5], refs[5:10]
    w_out, og_out, bias_out = refs[10:13]
    core = ids[0] & 1
    yy, xx = ids[1] & 3, ids[1] >> 2
    for j, off in enumerate((0, -1, 1, 2)):
        for i in range(2):
            k = j * 2 + i
            n, base = (j, i * 784) if j < 3 else (3 + i, 0)
            col = pl.multiple_of((((xx ^ i) << 2) | ((yy + off) & 3)) * B, B)
            for src, c in ((own[n], core), (other[n], 1 - core)):
                for m in range(4):
                    at = pl.multiple_of(c * 512 + m * B, B)
                    w_out[pl.ds(k * B, B), pl.ds(at, B)] = src[pl.ds(base + m * B, B), :]
            og_out[:, pl.ds(col, B)] = own[n][pl.ds(base + 512, 256), :]
            bias_out[:, pl.ds(col, B)] = own[n][pl.ds(base + 768, 16), :].astype(f32)[0:8]


def lay_out(ids, own, other):
    return pl.pallas_call(
        lay_body,
        out_shape=(
            jax.ShapeDtypeStruct((1024, 1024), bf16),
            jax.ShapeDtypeStruct((256, 1024), bf16),
            jax.ShapeDtypeStruct((8, 1024), f32),
        ),
        in_specs=[SM] + [VM] * 10,
        out_specs=(VM, VM, VM),
        compiler_params=params(),
        cost_estimate=cost(0, 5 << 20),
        name="lay_out",
    )(ids, *own, *other)


def mid_body(ids, p0, p1, p2, p3, w_full, og, bias, w_own, hidden, prop, keep, give, agg, pre, gp, wp):
    for j, p in enumerate((p0, p1, p2, p3)):
        for i in range(2):
            agg[:, (j * 2 + i) * B : (j * 2 + i + 1) * B] = p[i * 256 : (i + 1) * 256, :]
    for n in range(4):
        cols = slice(n * 256, (n + 1) * 256)
        v = jnp.dot(agg[...], w_full[:, cols], preferred_element_type=f32) + bias[0:1, cols]
        pre[:, cols] = v
        s = jax.nn.sigmoid(v)
        gp[:, cols] = (og[:, cols].astype(f32) * s * (1.0 + v * (1.0 - s))).astype(bf16)
    mine = pl.ds(pl.multiple_of(ids[1] * B, B), B)
    v = pre[:, mine]
    hidden[...] = v * jax.nn.sigmoid(v)
    prop[...] = lax.dot_general(
        gp[...], w_own[...], (((1,), (1,)), ((), ())), preferred_element_type=f32
    ).astype(bf16)
    wp[:, 0:1024] = lax.dot_general(
        agg[:, 0:B], gp[...], (((0,), (0,)), ((), ())), preferred_element_type=f32
    )
    total = jnp.sum(gp[:, mine].astype(f32), axis=0, keepdims=True)
    wp[:, 1024:1152] = jnp.broadcast_to(total, (B, B))
    x, core = ids[0] >> 4, ids[0] & 1
    for ref, c in ((keep, core), (give, 1 - core)):
        for i in range(2):
            ref[i * 32 : (i + 1) * 32, :] = wp[pl.ds(pl.multiple_of(c * 64 + (x ^ i) * 32, 32), 32), :]


def middle(ids, pieces, w_full, og, bias, w_own):
    return pl.pallas_call(
        mid_body,
        out_shape=(
            jax.ShapeDtypeStruct((256, B), f32),
            jax.ShapeDtypeStruct((256, B), bf16),
            jax.ShapeDtypeStruct((64, 1152), f32),
            jax.ShapeDtypeStruct((64, 1152), f32),
        ),
        in_specs=[SM] + [VM] * 8,
        out_specs=(VM, VM, VM, VM),
        scratch_shapes=[
            pltpu.VMEM((256, 1024), bf16),
            pltpu.VMEM((256, 1024), f32),
            pltpu.VMEM((256, 1024), bf16),
            pltpu.VMEM((B, 1152), f32),
        ],
        compiler_params=params(),
        cost_estimate=cost(2 * 256 * 1024 * 1280, 5 << 20),
        name="middle",
    )(ids, *pieces, w_full, og, bias, w_own)


def spread_body(ids, idx, dest, tiles, prop, keep0, keep1, give, acc):
    acc[...] = jnp.zeros_like(acc)
    core = ids[0] & 1

    def step(g, carry):
        for u in range(4):
            t = g * 4 + u
            i = idx[t]
            acc[i] += lax.dot_general(
                tiles[t], prop[dest[t]], (((0,), (0,)), ((), ())), preferred_element_type=f32
            )
        return carry

    lax.fori_loop(0, 16, step, 0)

    def take(dc, dz, dx):
        return acc[pl.ds(((dc * NZ + dz) * 2 + dx) * 2, 2)]

    for dx in range(2):
        ref = (keep0, keep1)[dx]
        for n, k in enumerate((3, 2, 1)):
            up = jnp.where(core == 0, k, NZ - k)
            ref[4 * n : 4 * n + 2] = take(0, up, dx)
            ref[4 * n + 2 : 4 * n + 4] = take(1, up, dx)
            at = 16 * dx + 4 * n
            give[at : at + 2] = take(1, NZ - up, dx).astype(bf16)
            give[at + 2 : at + 4] = take(0, NZ - up, dx).astype(bf16)
        for n, dz in ((12, 4), (14, 0)):
            ref[n : n + 2] = take(0, dz, dx)
            give[16 * dx + n : 16 * dx + n + 2] = take(1, dz, dx).astype(bf16)


def spread(ids, idx, dest, tiles, prop):
    return pl.pallas_call(
        spread_body,
        out_shape=(
            jax.ShapeDtypeStruct((16, B, B), f32),
            jax.ShapeDtypeStruct((16, B, B), f32),
            jax.ShapeDtypeStruct((32, B, B), bf16),
        ),
        in_specs=[SM, SM, SM, VM, VM],
        out_specs=(VM, VM, VM),
        scratch_shapes=[pltpu.VMEM((64, B, B), f32)],
        compiler_params=params(),
        cost_estimate=cost(2 * 64 * B**3, 6 << 20),
        name="spread",
    )(ids, idx, dest, tiles, prop)


def sum_body(scale, ids, own, d1, d2, d3, d4, e, out, buf):
    core, z = ids[0] & 1, (ids[0] >> 1) & 7
    buf[0] = own[...]
    buf[4] = d4[...]
    for k, d in ((1, d1), (2, d2), (3, d3)):
        mine = jnp.where(core == 0, NZ - k, k)
        buf[mine] = d[0:32, :]
        buf[NZ - mine] = e[(k - 1) * 32 : k * 32, :]
    acc = buf[(NZ - z) & 7].astype(f32)
    for n in range(1, NZ):
        acc = acc + buf[(n - z) & 7].astype(f32)
    out[...] = (acc * scale).astype(bf16)


def sum_z(scale, ids, *parts):
    return pl.pallas_call(
        functools.partial(sum_body, scale),
        out_shape=jax.ShapeDtypeStruct((32, 1152), bf16),
        in_specs=[SM] + [VM] * 6,
        out_specs=VM,
        scratch_shapes=[pltpu.VMEM((NZ, 32, 1152), bf16)],
        compiler_params=params(8),
        cost_estimate=cost(32 * 1152 * 8, 1 << 20),
        name="sum_z",
    )(ids, *parts)


def wout_body(ids, mine, theirs, w_out, b_out, buf):
    x, core = ids[0] >> 4, ids[0] & 1
    for ref, c in ((mine, core), (theirs, 1 - core)):
        for i in range(2):
            at = pl.multiple_of(c * 64 + (x ^ i) * 32, 32)
            buf[pl.ds(at, 32), :] = ref[i * 32 : (i + 1) * 32, :].astype(f32)
    w_out[...] = buf[:, 0:1024]
    b_out[...] = buf[0:8, 1024:1152]


def weight_out(ids, mine, theirs):
    return pl.pallas_call(
        wout_body,
        out_shape=(jax.ShapeDtypeStruct((B, 1024), f32), jax.ShapeDtypeStruct((8, B), f32)),
        in_specs=[SM, VM, VM],
        out_specs=(VM, VM),
        scratch_shapes=[pltpu.VMEM((B, 1152), f32)],
        compiler_params=params(8),
        cost_estimate=cost(0, 1 << 20),
        name="weight_out",
    )(ids, mine, theirs)


def body(features, weight, bias_vector, adj_tiles, col_blocks, dest_blocks, out_grad):
    me = lax.axis_index("row")
    my_x, my_z, my_c = me >> 4, (me >> 1) & 7, me & 1
    ids = jnp.stack([me, lax.axis_index("feat")]).astype(jnp.int32)
    owner = col_blocks >> 1
    ox, oz, oc = owner >> 4, (owner >> 1) & 7, owner & 1
    idx = ((((oc ^ my_c) * NZ + ((oz - my_z) & 7)) * 2 + (ox ^ my_x)) * 2) + (col_blocks & 1)

    both = jnp.concatenate([features, row_send(features, dc=1)], axis=0)
    x0 = row_send(features, dx=1)

    half = lax.dynamic_slice(weight, (0, my_c * 512), (B, 512))
    pack = jnp.concatenate(
        [half[:, m * B : (m + 1) * B] for m in range(4)]
        + [out_grad, jnp.broadcast_to(bias_vector[None, :], (16, B))],
        axis=0,
    )
    pair = jnp.concatenate([pack, feat_send(pack, dx=1)], axis=0)

    o1 = spin_send(both, 1)
    o2 = spin_send(both, 2)
    o3 = spin_send(after(both, pair), 3)
    o4 = row_send(features, dz=4)
    wu, wd = feat_send(pair, dy=1), feat_send(pair, dy=-1)
    p1, p2 = row_send(o1, dx=1), row_send(o2, dx=1)
    p3, p4 = row_send(after(o3, wu, wd), dx=1), row_send(o4, dx=1)
    wa, wb = feat_send(wu[:784], dy=1), feat_send(wd[784:], dy=-1)
    near = (both, x0, o4, o1, o2, o3, p4, p1, p2, p3)
    far = tuple(row_send(v, dc=1) for v in (x0, o4, o1, o2, o3, p4, p1, p2, p3))
    own = (pair, wu, wd, wa, wb)
    other = tuple(row_send(v, dc=1) for v in own)

    aggregated = aggregate(ids, idx, dest_blocks, adj_tiles, near, far)

    q = jnp.concatenate([aggregated, feat_send(after(aggregated, wa, wb), dx=1)], axis=0)
    w_full, og, bias = lay_out(ids, own, other)
    q2 = after(q, w_full)
    pieces = (q, feat_send(q2, dy=1), feat_send(q2, dy=-1), feat_send(q2, dy=2))
    hidden, prop, keep, give = middle(ids, pieces, w_full, og, bias, weight)

    got = row_send(give, dc=1)
    more = row_send((keep[32:] + got[32:]).astype(bf16), dx=1)

    keep0, keep1, away = spread(ids, idx, dest_blocks, adj_tiles, prop.reshape(2, B, B))
    came = row_send(away, dc=1).astype(f32)
    half0, half1 = keep0 + came[:16], (keep1 + came[16:]).astype(bf16)
    xa = row_send(half1[:8], dx=1)
    xb = row_send(half1[8:], dx=1)

    quarter = (keep[:32] + got[:32] + more.astype(f32)).astype(bf16)
    halves = after(jnp.concatenate([quarter, row_send(quarter, dc=1)], axis=0), half1)
    d1, d2, d3 = (spin_send(halves, k) for k in (1, 2, 3))
    d4 = row_send(quarter, dz=4)

    ta = (half0[:8] + xa.astype(f32)).astype(bf16)
    tb = half0[8:] + xb.astype(f32)
    r3, r2 = spin_send(ta[:4], 3), spin_send(ta[4:], 2)
    r1 = spin_send(tb[:4].astype(bf16), 1)
    r4 = row_send(tb[4:6].astype(bf16), dz=4)

    e = row_send(after(jnp.concatenate([d1[32:], d2[32:], d3[32:]], axis=0), ta, tb), dc=1)
    scale = float(256 * lax.axis_size("row")) ** (-0.5)
    total = sum_z(scale, ids, quarter, d1, d2, d3, d4, e)
    two = jnp.concatenate([total, row_send(total, dx=1)], axis=0)
    weight_grad, bias_grad = weight_out(ids, two, row_send(two, dc=1))

    r = r1.astype(f32) + r2.astype(f32) + r3.astype(f32)
    out = tb[6:] + r4.astype(f32) + r[:2] + row_send(r[2:], dc=1)
    return hidden, out.reshape(256, B), weight_grad, bias_grad[0]


def solution(mesh):
    in_specs = (
        P("row", "feat"),
        P("feat", None),
        P("feat"),
        P("row", None, None),
        P("row"),
        P("row"),
        P("row", "feat"),
    )
    out_specs = (P("row", "feat"), P("row", "feat"), P("feat", None), P("feat"))
    return jax.shard_map(body, mesh=mesh, in_specs=in_specs, out_specs=out_specs, check_vma=False)
```

time: 192 us -> 146 us (0.76)
  waiting for transfers between devices: 50.5 us -> 32.2 us
  between operations: 16.1 us -> 0.93 us
  other arithmetic: 8.36 us -> 1.61 us
  local copies, waits for them, and re-layouts: 21 us -> 17.3 us
    ppermute x33, waiting for transfers between devices: 35.7 us -> 14.9 us  [row_send(): return lax.ppermute(v, 'row', perm)]
    ppermute x33, starting transfers between devices: 65.7 us -> 47 us  [row_send(): return lax.ppermute(v, 'row', perm)]
    ppermute x0 -> x9, starting transfers between devices: none -> 14.5 us  [spin_send(): return lax.ppermute(v, 'row', perm)]
    ppermute x0 -> x9, waiting for transfers between devices: none -> 9.7 us  [spin_send(): return lax.ppermute(v, 'row', perm)]
    ppermute x8 -> x9, waiting for transfers between devices: 14.7 us -> 7.63 us  [feat_send(): lax.ppermute(v, 'feat', [(i, (i >> 2 ^ dx) << 2 | i + dy & 3) for i in ra...]
    ppermute x8 -> x9, starting transfers between devices: 12.4 us -> 15.7 us  [feat_send(): lax.ppermute(v, 'feat', [(i, (i >> 2 ^ dx) << 2 | i + dy & 3) for i in ra...]
    unnamed x51 -> x37, local copies, waits for them, and re-layouts: 17 us -> 14.6 us
    add x3 -> x2, other arithmetic: 2.96 us -> 0.74 us  [the longest x1 0.69 us: body(): out = tb[6:] + r4.astype(f32) + r[:2] + row_send(r[2:], dc=1)]
  transfers between devices with their start and end apart: 41 -> 51, of which waited for: 20 -> 13; matrix products, arithmetic and copies ran while one was open for 8% -> 2% of each run, Pallas kernels for 7% -> 7%
where the time goes in v2:
time: 146 us; the launch traced here: 145 us
  starting transfers between devices  77.2 us (53%)
  waiting for transfers between devices  32.2 us (22%)
  local copies, waits for them, and re-layouts  17.3 us (12%)
  Pallas kernels  15.8 us (11%)
  other arithmetic  1.61 us (1%)
    ppermute x33, starting transfers between devices, row_send(): return lax.ppermute(v, 'row', perm)  47 us
    ppermute x9, starting transfers between devices, feat_send(): lax.ppermute(v, 'feat', [(i, (i >> 2 ^ dx) << 2 | i + dy & 3) for i in ra...  15.7 us
    ppermute x33, waiting for transfers between devices, row_send(): return lax.ppermute(v, 'row', perm)  14.9 us
    unnamed x37, local copies, waits for them, and re-layouts  14.6 us
    ppermute x9, starting transfers between devices, spin_send(): return lax.ppermute(v, 'row', perm)  14.5 us
    ppermute x9, waiting for transfers between devices, spin_send(): return lax.ppermute(v, 'row', perm)  9.7 us
    ppermute x9, waiting for transfers between devices, feat_send(): lax.ppermute(v, 'feat', [(i, (i >> 2 ^ dx) << 2 | i + dy & 3) for i in ra...  7.63 us
    pallas_call x1, Pallas kernels, aggregate(): pl.pallas_call(agg_body, out_shape=jax.ShapeDtypeStruct((2 * B, B), bf16)...  5.23 us
  transfers between devices with their start and end apart: 51, of which 13 were waited for; matrix products, arithmetic and copies ran while one was open for 2% of the time, Pallas kernels for 7%

profile of v2, /device:TPU:1, one launch (start us, length us, event | category | flops | bytes accessed | tf_op | source)
XLA Modules:
  0.0 145.0 jit_solution(15526807024584710340)
XLA Ops:
  0.7 0.9 constant_dynamic-update-slice_fusion.7
  6.2 0.9 constant_dynamic-update-slice_fusion.3
  7.7 3.6 %collective-permute-start.5 = (bf16[784,128]{1,0:T(8,128)(2,1)S(1)}, bf16[784,128]{1,0:T(8,128)(2,1)S(1)}, u32[]{:S(2)}, u32[]{:S(2)}) collective-permute-start(bf16[784,128]{1,0:T(8,128)(2,1)S(1)} %get-tuple-element.53), channel_id=1, source_target_pairs={{0,4},{1,5},{2,6},{3,7},{4,0},{5,1},{6,2},{7,3},{8,12},{9,13},{10,... | collective-permute-start | bytes 602120 | tf_op jit(solution)/shard_map/ppermute | solution.py:27
  11.3 1.0 collective-permute-start
  12.3 6.9 %collective-permute-start.2 = (bf16[256,128]{1,0:T(8,128)(2,1)}, bf16[256,128]{1,0:T(8,128)(2,1)S(1)}, u32[]{:S(2)}, u32[]{:S(2)}) collective-permute-start(bf16[256,128]{1,0:T(8,128)(2,1)} %param.7), channel_id=1, source_target_pairs={{0,64},{8,72},{16,80},{24,88},{32,96},{40,104},{48,112},{56,120},{... | collective-permute-start | bytes 196616 | tf_op jit(solution)/shard_map/ppermute | solution.py:23
  19.5 1.4 collective-permute-start.10
  20.9 1.5 %collective-permute-start.11 = (bf16[1568,128]{1,0:T(8,128)(2,1)S(1)}, bf16[1568,128]{1,0:T(8,128)(2,1)S(1)}, u32[]{:S(2)}, u32[]{:S(2)}) collective-permute-start(bf16[1568,128]{1,0:T(8,128)(2,1)S(1)} %constant_dynamic-update-slice_fusion.8.refs_0_), channel_id=1, source_target_pairs={{0,3},{1,0},{2,1},{3,2},{4,7},{5,4},{6,5},{7,6},{8,11},{9,8},{10,9... | collective-permute-start | bytes 1204232 | tf_op jit(solution)/shard_map/ppermute | solution.py:27
  23.3 1.2 collective-permute-start.7
  24.5 2.1 %collective-permute-start.3 = (bf16[512,128]{1,0:T(8,128)(2,1)S(1)}, bf16[512,128]{1,0:T(8,128)(2,1)}, u32[]{:S(2)}, u32[]{:S(2)}) collective-permute-start(bf16[512,128]{1,0:T(8,128)(2,1)S(1)} %constant_dynamic-update-slice_fusion), channel_id=1, source_target_pairs={{0,16},{8,120},{16,32},{24,8},{32,48},{40,24},{48,64},{56,40},{64,... | collective-permute-start | bytes 393224 | tf_op jit(solution)/shard_map/ppermute | solution.py:39
  26.6 1.4 collective-permute-start.4
  28.0 2.0 %collective-permute-start.6 = (bf16[512,128]{1,0:T(8,128)(2,1)S(1)}, bf16[512,128]{1,0:T(8,128)(2,1)}, u32[]{:S(2)}, u32[]{:S(2)}) collective-permute-start(bf16[512,128]{1,0:T(8,128)(2,1)S(1)} %constant_dynamic-update-slice_fusion), channel_id=1, source_target_pairs={{0,48},{8,88},{16,64},{24,104},{32,80},{40,120},{48,96},{56,8},{64... | collective-permute-start | bytes 393224 | tf_op jit(solution)/shard_map/ppermute | solution.py:39
  30.8 1.7 %collective-permute-done.4 = bf16[512,128]{1,0:T(8,128)(2,1)} collective-permute-done((bf16[512,128]{1,0:T(8,128)(2,1)S(1)}, bf16[512,128]{1,0:T(8,128)(2,1)}, u32[]{:S(2)}, u32[]{:S(2)}) %collective-permute-start.4) | collective-permute-done | bytes 131104 | tf_op jit(solution)/shard_map/ppermute | solution.py:39
  32.5 3.9 %collective-permute-start.14 = (bf16[256,128]{1,0:T(8,128)(2,1)S(1)}, bf16[256,128]{1,0:T(8,128)(2,1)S(1)}, u32[]{:S(2)}, u32[]{:S(2)}) collective-permute-start(bf16[256,128]{1,0:T(8,128)(2,1)S(1)} %collective-permute-done.2), channel_id=1, source_target_pairs={{0,8},{8,0},{16,24},{24,16},{32,40},{40,32},{48,56},{56,48},{64,72... | collective-permute-start | bytes 196616 | tf_op jit(solution)/shard_map/ppermute | solution.py:23
  36.4 5.5 %collective-permute-start.13 = (bf16[256,128]{1,0:T(8,128)(2,1)S(1)}, bf16[256,128]{1,0:T(8,128)(2,1)S(1)}, u32[]{:S(2)}, u32[]{:S(2)}) collective-permute-start(bf16[256,128]{1,0:T(8,128)(2,1)S(1)} %collective-permute-done.1), channel_id=1, source_target_pairs={{0,8},{8,0},{16,24},{24,16},{32,40},{40,32},{48,56},{56,48},{64,72... | collective-permute-start | bytes 196616 | tf_op jit(solution)/shard_map/ppermute | solution.py:23
  46.0 1.7 %collective-permute-start.12 = (bf16[512,128]{1,0:T(8,128)(2,1)}, bf16[512,128]{1,0:T(8,128)(2,1)}, u32[]{:S(2)}, u32[]{:S(2)}) collective-permute-start(bf16[512,128]{1,0:T(8,128)(2,1)} %collective-permute-done.6), channel_id=1, source_target_pairs={{0,128},{8,136},{16,144},{24,152},{32,160},{40,168},{48,176},{56,1... | collective-permute-start | bytes 393224 | tf_op jit(solution)/shard_map/ppermute | solution.py:23
  49.9 2.4 %collective-permute-start.23 = (bf16[784,128]{1,0:T(8,128)(2,1)}, bf16[784,128]{1,0:T(8,128)(2,1)}, u32[]{:S(2)}, u32[]{:S(2)}) collective-permute-start(bf16[784,128]{1,0:T(8,128)(2,1)} %slice.111), channel_id=1, source_target_pairs={{0,3},{1,0},{2,1},{3,2},{4,7},{5,4},{6,5},{7,6},{8,11},{9,8},{10,9... | collective-permute-start | bytes 602120 | tf_op jit(solution)/shard_map/ppermute | solution.py:27
  52.3 0.8 collective-permute-start.21
  59.1 5.2 %aggregate.1 = bf16[256,128]{1,0:T(8,128)(2,1)S(1)} custom-call(s32[2]{0:T(128)S(1)} %pad_add_fusion.ids, s32[64]{0:T(128)S(1)} %and_add_fusion.idx, s32[64]{0:T(128)S(1)} %copy-done.12, bf16[64,128,128]{2,1,0:T(8,128)(2,1)S(1)} %copy-done, bf16[4,128,128]{2,1,0:T(8,128)(2,1)S(1)} %bitcast.25, bf16[2,128,128]{2,1,0:T(8,128)(2,1)S(1)} %bitcast.27, ...), custom_call_target="tpu_custom_call" | custom-call | flops 268435456 | bytes 4194304 | tf_op jit(solution)/shard_map/aggregate/pallas_call | solution.py:95
  64.4 2.6 %collective-permute-start.24 = (bf16[256,128]{1,0:T(8,128)(2,1)S(1)}, bf16[256,128]{1,0:T(8,128)(2,1)S(1)}, u32[]{:S(2)}, u32[]{:S(2)}) collective-permute-start(bf16[256,128]{1,0:T(8,128)(2,1)S(1)} %aggregate.1), channel_id=1, source_target_pairs={{0,4},{1,5},{2,6},{3,7},{4,0},{5,1},{6,2},{7,3},{8,12},{9,13},{10,... | collective-permute-start | bytes 196616 | tf_op jit(solution)/shard_map/ppermute | solution.py:27
  67.4 2.1 %collective-permute-done.24 = bf16[256,128]{1,0:T(8,128)(2,1)S(1)} collective-permute-done((bf16[256,128]{1,0:T(8,128)(2,1)S(1)}, bf16[256,128]{1,0:T(8,128)(2,1)S(1)}, u32[]{:S(2)}, u32[]{:S(2)}) %collective-permute-start.24) | collective-permute-done | bytes 65568 | tf_op jit(solution)/shard_map/ppermute | solution.py:27
  69.5 1.0 collective-permute-start.29
  70.5 1.3 collective-permute-done.29.refs_9_
  71.8 1.7 %lay_out.1 = (bf16[1024,1024]{1,0:T(8,128)(2,1)S(1)}, bf16[256,1024]{1,0:T(8,128)(2,1)S(1)}, f32[8,1024]{1,0:T(8,128)S(1)}) custom-call(s32[2]{0:T(128)S(1)} %pad_add_fusion.ids, bf16[1568,128]{1,0:T(8,128)(2,1)S(1)} %constant_dynamic-update-slice_fusion.8.refs_0_, bf16[1568,128]{1,0:T(8,128)(2,1)S(1)} %collective-permute-done.10.refs_1_, ...), custom_call_target="tpu_custom_call" | custom-call | bytes 5242880 | tf_op jit(solution)/shard_map/lay_out/pallas_call | solution.py:126
  73.5 0.9 collective-permute-start.30
  74.4 1.9 %collective-permute-start.31 = (bf16[512,128]{1,0:T(8,128)(2,1)S(1)}, bf16[512,128]{1,0:T(8,128)(2,1)S(1)}, u32[]{:S(2)}, u32[]{:S(2)}) collective-permute-start(bf16[512,128]{1,0:T(8,128)(2,1)S(1)} %pad_maximum_fusion.3.p0), channel_id=1, source_target_pairs={{0,3},{1,0},{2,1},{3,2},{4,7},{5,4},{6,5},{7,6},{8,11},{9,8},{10,9... | collective-permute-start | bytes 393224 | tf_op jit(solution)/shard_map/ppermute | solution.py:27
  76.3 1.2 collective-permute-start.32
  77.5 2.1 %collective-permute-done.30.p1 = bf16[512,128]{1,0:T(8,128)(2,1)S(1)} collective-permute-done((bf16[512,128]{1,0:T(8,128)(2,1)S(1)}, bf16[512,128]{1,0:T(8,128)(2,1)S(1)}, u32[]{:S(2)}, u32[]{:S(2)}) %collective-permute-start.30) | collective-permute-done | bytes 131104 | tf_op jit(solution)/shard_map/ppermute | solution.py:27
  79.5 3.4 %collective-permute-done.32.p3 = bf16[512,128]{1,0:T(8,128)(2,1)S(1)} collective-permute-done((bf16[512,128]{1,0:T(8,128)(2,1)S(1)}, bf16[512,128]{1,0:T(8,128)(2,1)S(1)}, u32[]{:S(2)}, u32[]{:S(2)}) %collective-permute-start.32) | collective-permute-done | bytes 131104 | tf_op jit(solution)/shard_map/ppermute | solution.py:27
  83.0 2.2 %middle.1 = (f32[256,128]{1,0:T(8,128)}, bf16[256,128]{1,0:T(8,128)(2,1)S(1)}, f32[64,1152]{1,0:T(8,128)S(1)}, f32[64,1152]{1,0:T(8,128)S(1)}) custom-call(s32[2]{0:T(128)S(1)} %pad_add_fusion.ids, bf16[512,128]{1,0:T(8,128)(2,1)S(1)} %pad_maximum_fusion.3.p0, bf16[512,128]{1,0:T(8,128)(2,1)S(1)} %collective-permute-done.30.p1, ...), custom_call_target="tpu_custom_call" | custom-call | flops 671088640 | bytes 5242880 | tf_op jit(solution)/shard_map/middle/pallas_call | solution.py:169
  85.1 1.3 collective-permute-start.41
  86.4 4.6 %spread.1 = (f32[16,128,128]{2,1,0:T(8,128)S(1)}, f32[16,128,128]{2,1,0:T(8,128)S(1)}, bf16[32,128,128]{2,1,0:T(8,128)(2,1)S(1)}) custom-call(s32[2]{0:T(128)S(1)} %pad_add_fusion.ids, s32[64]{0:T(128)S(1)} %and_add_fusion.idx, s32[64]{0:T(128)S(1)} %copy-done.12, bf16[64,128,128]{2,1,0:T(8,128)(2,1)S(1)} %copy-done, bf16[2,128,128]{2,1,0:T(8,128)(2,1)S(1)} %bitcast.32), custom_call_target="tpu_custom_call" | custom-call | flops 268435456 | bytes 6291456 | tf_op jit(solution)/shard_map/spread/pallas_call | solution.py:224
  91.8 2.9 %collective-permute-done.42 = bf16[32,1152]{1,0:T(8,128)(2,1)S(1)} collective-permute-done((bf16[32,1152]{1,0:T(8,128)(2,1)S(1)}, bf16[32,1152]{1,0:T(8,128)(2,1)S(1)}, u32[]{:S(2)}, u32[]{:S(2)}) %collective-permute-start.42) | collective-permute-done | bytes 73760 | tf_op jit(solution)/shard_map/ppermute | solution.py:23
  94.7 1.7 %collective-permute-start.43 = (bf16[32,1152]{1,0:T(8,128)(2,1)S(1)}, bf16[32,1152]{1,0:T(8,128)(2,1)S(1)}, u32[]{:S(2)}, u32[]{:S(2)}) collective-permute-start(bf16[32,1152]{1,0:T(8,128)(2,1)S(1)} %fusion.4.own), channel_id=1, source_target_pairs={{0,8},{8,0},{16,24},{24,16},{32,40},{40,32},{48,56},{56,48},{64,72... | collective-permute-start | bytes 221192 | tf_op jit(solution)/shard_map/ppermute | solution.py:23
  96.5 0.9 collective-permute-done.43
  98.0 3.0 %collective-permute-start.45 = (bf16[64,1152]{1,0:T(8,128)(2,1)S(1)}, bf16[64,1152]{1,0:T(8,128)(2,1)S(1)}, u32[]{:S(2)}, u32[]{:S(2)}) collective-permute-start(bf16[64,1152]{1,0:T(8,128)(2,1)S(1)} %pad_maximum_fusion.1), channel_id=1, source_target_pairs={{0,32},{8,104},{16,48},{24,120},{32,64},{40,8},{48,80},{56,24},{64... | collective-permute-start | bytes 442376 | tf_op jit(solution)/shard_map/ppermute | solution.py:39
  101.9 1.0 collective-permute-start.37
  102.9 4.1 %collective-permute-done.45.d2 = bf16[64,1152]{1,0:T(8,128)(2,1)S(1)} collective-permute-done((bf16[64,1152]{1,0:T(8,128)(2,1)S(1)}, bf16[64,1152]{1,0:T(8,128)(2,1)S(1)}, u32[]{:S(2)}, u32[]{:S(2)}) %collective-permute-start.45) | collective-permute-done | bytes 147488 | tf_op jit(solution)/shard_map/ppermute | solution.py:39
  107.0 3.9 %collective-permute-done.46.d3 = bf16[64,1152]{1,0:T(8,128)(2,1)S(1)} collective-permute-done((bf16[64,1152]{1,0:T(8,128)(2,1)S(1)}, bf16[64,1152]{1,0:T(8,128)(2,1)S(1)}, u32[]{:S(2)}, u32[]{:S(2)}) %collective-permute-start.46) | collective-permute-done | bytes 147488 | tf_op jit(solution)/shard_map/ppermute | solution.py:39
  111.0 2.3 %collective-permute-done.37 = bf16[8,128,128]{2,1,0:T(8,128)(2,1)S(1)} collective-permute-done((bf16[8,128,128]{2,1,0:T(8,128)(2,1)S(1)}, bf16[8,128,128]{2,1,0:T(8,128)(2,1)S(1)}, u32[]{:S(2)}, u32[]{:S(2)}) %collective-permute-start.37) | collective-permute-done | bytes 262176 | tf_op jit(solution)/shard_map/ppermute | solution.py:23
  113.4 2.6 %collective-permute-start.48 = (bf16[96,1152]{1,0:T(8,128)(2,1)S(1)}, bf16[96,1152]{1,0:T(8,128)(2,1)S(1)}, u32[]{:S(2)}, u32[]{:S(2)}) collective-permute-start(bf16[96,1152]{1,0:T(8,128)(2,1)S(1)} %pad_maximum_fusion), channel_id=1, source_target_pairs={{0,8},{8,0},{16,24},{24,16},{32,40},{40,32},{48,56},{56,48},{64,72... | collective-permute-start | bytes 663560 | tf_op jit(solution)/shard_map/ppermute | solution.py:23
  116.0 2.7 %collective-permute-start.38 = (bf16[4,128,128]{2,1,0:T(8,128)(2,1)S(1)}, bf16[4,128,128]{2,1,0:T(8,128)(2,1)S(1)}, u32[]{:S(2)}, u32[]{:S(2)}) collective-permute-start(bf16[4,128,128]{2,1,0:T(8,128)(2,1)S(1)} %get-tuple-element.47), channel_id=1, source_target_pairs={{0,32},{8,104},{16,48},{24,120},{32,64},{40,8},{48,80},{56,24},{64... | collective-permute-start | bytes 393224 | tf_op jit(solution)/shard_map/ppermute | solution.py:39
  118.8 2.7 %collective-permute-start.39 = (bf16[4,128,128]{2,1,0:T(8,128)(2,1)S(1)}, bf16[4,128,128]{2,1,0:T(8,128)(2,1)S(1)}, u32[]{:S(2)}, u32[]{:S(2)}) collective-permute-start(bf16[4,128,128]{2,1,0:T(8,128)(2,1)S(1)} %get-tuple-element.48), channel_id=1, source_target_pairs={{0,48},{8,88},{16,64},{24,104},{32,80},{40,120},{48,96},{56,8},{64... | collective-permute-start | bytes 393224 | tf_op jit(solution)/shard_map/ppermute | solution.py:39
  121.6 2.9 %collective-permute-start.47 = (bf16[32,1152]{1,0:T(8,128)(2,1)S(1)}, bf16[32,1152]{1,0:T(8,128)(2,1)S(1)}, u32[]{:S(2)}, u32[]{:S(2)}) collective-permute-start(bf16[32,1152]{1,0:T(8,128)(2,1)S(1)} %fusion.4.own), channel_id=1, source_target_pairs={{0,64},{8,72},{16,80},{24,88},{32,96},{40,104},{48,112},{56,120},{... | collective-permute-start | bytes 221192 | tf_op jit(solution)/shard_map/ppermute | solution.py:23
  124.5 6.5 %collective-permute-done.47.d4 = bf16[32,1152]{1,0:T(8,128)(2,1)S(1)} collective-permute-done((bf16[32,1152]{1,0:T(8,128)(2,1)S(1)}, bf16[32,1152]{1,0:T(8,128)(2,1)S(1)}, u32[]{:S(2)}, u32[]{:S(2)}) %collective-permute-start.47) | collective-permute-done | bytes 73760 | tf_op jit(solution)/shard_map/ppermute | solution.py:23
  131.0 2.9 %collective-permute-start.35 = (bf16[2,128,128]{2,1,0:T(8,128)(2,1)S(1)}, bf16[2,128,128]{2,1,0:T(8,128)(2,1)S(1)}, u32[]{:S(2)}, u32[]{:S(2)}) collective-permute-start(bf16[2,128,128]{2,1,0:T(8,128)(2,1)S(1)} %slice.117), channel_id=1, source_target_pairs={{0,64},{8,72},{16,80},{24,88},{32,96},{40,104},{48,112},{56,120},{... | collective-permute-start | bytes 196616 | tf_op jit(solution)/shard_map/ppermute | solution.py:23
  135.1 3.5 %collective-permute-start.40 = (f32[2,128,128]{2,1,0:T(8,128)S(1)}, f32[2,128,128]{2,1,0:T(8,128)S(1)}, u32[]{:S(2)}, u32[]{:S(2)}) collective-permute-start(f32[2,128,128]{2,1,0:T(8,128)S(1)} %slice.124), channel_id=1, source_target_pairs={{0,8},{8,0},{16,24},{24,16},{32,40},{40,32},{48,56},{56,48},{64,72... | collective-permute-start | bytes 393224 | tf_op jit(solution)/shard_map/ppermute | solution.py:23
  138.6 3.5 %collective-permute-start.50 = (bf16[64,1152]{1,0:T(8,128)(2,1)S(1)}, bf16[64,1152]{1,0:T(8,128)(2,1)S(1)}, u32[]{:S(2)}, u32[]{:S(2)}) collective-permute-start(bf16[64,1152]{1,0:T(8,128)(2,1)S(1)} %pad_maximum_fusion.2.mine), channel_id=1, source_target_pairs={{0,8},{8,0},{16,24},{24,16},{32,40},{40,32},{48,56},{56,48},{64,72... | collective-permute-start | bytes 442376 | tf_op jit(solution)/shard_map/ppermute | solution.py:23
  143.1 1.4 weight_out.1
  (124 shorter events, 25.5 us)
Async XLA Ops:
  7.7 11.8 %collective-permute-start.5 = (bf16[784,128]{1,0:T(8,128)(2,1)S(1)}, bf16[784,128]{1,0:T(8,128)(2,1)S(1)}, u32[]{:S(2)}, u32[]{:S(2)}) collective-permute-start(bf16[784,128]{1,0:T(8,128)(2,1)S(1)} %get-tuple-element.53), channel_id=1, source_target_pairs={{0,4},{1,5},{2,6},{3,7},{4,0},{5,1},{6,2},{7,3},{8,12},{9,13},{10,... | collective-permute-start | bytes 602120 | tf_op jit(solution)/shard_map/ppermute | solution.py:27
  11.3 13.1 %collective-permute-start = (bf16[256,128]{1,0:T(8,128)(2,1)}, bf16[256,128]{1,0:T(8,128)(2,1)S(1)}, u32[]{:S(2)}, u32[]{:S(2)}) collective-permute-start(bf16[256,128]{1,0:T(8,128)(2,1)} %param.7), channel_id=1, source_target_pairs={{0,8},{8,0},{16,24},{24,16},{32,40},{40,32},{48,56},{56,48},{64,72... | collective-permute-start | bytes 196616 | tf_op jit(solution)/shard_map/ppermute | solution.py:23
  12.3 11.0 %collective-permute-start.2 = (bf16[256,128]{1,0:T(8,128)(2,1)}, bf16[256,128]{1,0:T(8,128)(2,1)S(1)}, u32[]{:S(2)}, u32[]{:S(2)}) collective-permute-start(bf16[256,128]{1,0:T(8,128)(2,1)} %param.7), channel_id=1, source_target_pairs={{0,64},{8,72},{16,80},{24,88},{32,96},{40,104},{48,112},{56,120},{... | collective-permute-start | bytes 196616 | tf_op jit(solution)/shard_map/ppermute | solution.py:23
  19.2 7.4 %collective-permute-start.1 = (bf16[256,128]{1,0:T(8,128)(2,1)}, bf16[256,128]{1,0:T(8,128)(2,1)S(1)}, u32[]{:S(2)}, u32[]{:S(2)}) collective-permute-start(bf16[256,128]{1,0:T(8,128)(2,1)} %param.7), channel_id=1, source_target_pairs={{0,128},{8,136},{16,144},{24,152},{32,160},{40,168},{48,176},{56,1... | collective-permute-start | bytes 196616 | tf_op jit(solution)/shard_map/ppermute | solution.py:23
  19.5 22.9 %collective-permute-start.10 = (bf16[1568,128]{1,0:T(8,128)(2,1)S(1)}, bf16[1568,128]{1,0:T(8,128)(2,1)S(1)}, u32[]{:S(2)}, u32[]{:S(2)}) collective-permute-start(bf16[1568,128]{1,0:T(8,128)(2,1)S(1)} %constant_dynamic-update-slice_fusion.8.refs_0_), channel_id=1, source_target_pairs={{0,1},{1,2},{2,3},{3,0},{4,5},{5,6},{6,7},{7,4},{8,9},{9,10},{10,1... | collective-permute-start | bytes 1204232 | tf_op jit(solution)/shard_map/ppermute | solution.py:27
  20.9 22.2 %collective-permute-start.11 = (bf16[1568,128]{1,0:T(8,128)(2,1)S(1)}, bf16[1568,128]{1,0:T(8,128)(2,1)S(1)}, u32[]{:S(2)}, u32[]{:S(2)}) collective-permute-start(bf16[1568,128]{1,0:T(8,128)(2,1)S(1)} %constant_dynamic-update-slice_fusion.8.refs_0_), channel_id=1, source_target_pairs={{0,3},{1,0},{2,1},{3,2},{4,7},{5,4},{6,5},{7,6},{8,11},{9,8},{10,9... | collective-permute-start | bytes 1204232 | tf_op jit(solution)/shard_map/ppermute | solution.py:27
  23.3 4.7 %collective-permute-start.7 = (bf16[256,128]{1,0:T(8,128)(2,1)S(1)}, bf16[256,128]{1,0:T(8,128)(2,1)S(1)}, u32[]{:S(2)}, u32[]{:S(2)}) collective-permute-start(bf16[256,128]{1,0:T(8,128)(2,1)S(1)} %collective-permute-done.2), channel_id=1, source_target_pairs={{0,128},{8,136},{16,144},{24,152},{32,160},{40,168},{48,176},{56,1... | collective-permute-start | bytes 196616 | tf_op jit(solution)/shard_map/ppermute | solution.py:23
  24.5 5.5 %collective-permute-start.3 = (bf16[512,128]{1,0:T(8,128)(2,1)S(1)}, bf16[512,128]{1,0:T(8,128)(2,1)}, u32[]{:S(2)}, u32[]{:S(2)}) collective-permute-start(bf16[512,128]{1,0:T(8,128)(2,1)S(1)} %constant_dynamic-update-slice_fusion), channel_id=1, source_target_pairs={{0,16},{8,120},{16,32},{24,8},{32,48},{40,24},{48,64},{56,40},{64,... | collective-permute-start | bytes 393224 | tf_op jit(solution)/shard_map/ppermute | solution.py:39
  26.6 5.9 %collective-permute-start.4 = (bf16[512,128]{1,0:T(8,128)(2,1)S(1)}, bf16[512,128]{1,0:T(8,128)(2,1)}, u32[]{:S(2)}, u32[]{:S(2)}) collective-permute-start(bf16[512,128]{1,0:T(8,128)(2,1)S(1)} %constant_dynamic-update-slice_fusion), channel_id=1, source_target_pairs={{0,32},{8,104},{16,48},{24,120},{32,64},{40,8},{48,80},{56,24},{64... | collective-permute-start | bytes 393224 | tf_op jit(solution)/shard_map/ppermute | solution.py:39
  28.0 8.4 %collective-permute-start.6 = (bf16[512,128]{1,0:T(8,128)(2,1)S(1)}, bf16[512,128]{1,0:T(8,128)(2,1)}, u32[]{:S(2)}, u32[]{:S(2)}) collective-permute-start(bf16[512,128]{1,0:T(8,128)(2,1)S(1)} %constant_dynamic-update-slice_fusion), channel_id=1, source_target_pairs={{0,48},{8,88},{16,64},{24,104},{32,80},{40,120},{48,96},{56,8},{64... | collective-permute-start | bytes 393224 | tf_op jit(solution)/shard_map/ppermute | solution.py:39
  30.0 14.9 %collective-permute-start.8 = (bf16[512,128]{1,0:T(8,128)(2,1)}, bf16[512,128]{1,0:T(8,128)(2,1)}, u32[]{:S(2)}, u32[]{:S(2)}) collective-permute-start(bf16[512,128]{1,0:T(8,128)(2,1)} %collective-permute-done.3), channel_id=1, source_target_pairs={{0,128},{8,136},{16,144},{24,152},{32,160},{40,168},{48,176},{56,1... | collective-permute-start | bytes 393224 | tf_op jit(solution)/shard_map/ppermute | solution.py:23
  32.5 10.6 %collective-permute-start.14 = (bf16[256,128]{1,0:T(8,128)(2,1)S(1)}, bf16[256,128]{1,0:T(8,128)(2,1)S(1)}, u32[]{:S(2)}, u32[]{:S(2)}) collective-permute-start(bf16[256,128]{1,0:T(8,128)(2,1)S(1)} %collective-permute-done.2), channel_id=1, source_target_pairs={{0,8},{8,0},{16,24},{24,16},{32,40},{40,32},{48,56},{56,48},{64,72... | collective-permute-start | bytes 196616 | tf_op jit(solution)/shard_map/ppermute | solution.py:23
  36.4 7.9 %collective-permute-start.13 = (bf16[256,128]{1,0:T(8,128)(2,1)S(1)}, bf16[256,128]{1,0:T(8,128)(2,1)S(1)}, u32[]{:S(2)}, u32[]{:S(2)}) collective-permute-start(bf16[256,128]{1,0:T(8,128)(2,1)S(1)} %collective-permute-done.1), channel_id=1, source_target_pairs={{0,8},{8,0},{16,24},{24,16},{32,40},{40,32},{48,56},{56,48},{64,72... | collective-permute-start | bytes 196616 | tf_op jit(solution)/shard_map/ppermute | solution.py:23
  42.4 2.9 %collective-permute-start.18 = (bf16[256,128]{1,0:T(8,128)(2,1)S(1)}, bf16[256,128]{1,0:T(8,128)(2,1)S(1)}, u32[]{:S(2)}, u32[]{:S(2)}) collective-permute-start(bf16[256,128]{1,0:T(8,128)(2,1)S(1)} %collective-permute-done.7), channel_id=1, source_target_pairs={{0,8},{8,0},{16,24},{24,16},{32,40},{40,32},{48,56},{56,48},{64,72... | collective-permute-start | bytes 196616 | tf_op jit(solution)/shard_map/ppermute | solution.py:23
  43.1 6.0 %collective-permute-start.9 = (bf16[512,128]{1,0:T(8,128)(2,1)}, bf16[512,128]{1,0:T(8,128)(2,1)}, u32[]{:S(2)}, u32[]{:S(2)}) collective-permute-start(bf16[512,128]{1,0:T(8,128)(2,1)} %collective-permute-done.4), channel_id=1, source_target_pairs={{0,128},{8,136},{16,144},{24,152},{32,160},{40,168},{48,176},{56,1... | collective-permute-start | bytes 393224 | tf_op jit(solution)/shard_map/ppermute | solution.py:23
  43.7 5.7 %collective-permute-start.15 = (bf16[512,128]{1,0:T(8,128)(2,1)}, bf16[512,128]{1,0:T(8,128)(2,1)}, u32[]{:S(2)}, u32[]{:S(2)}) collective-permute-start(bf16[512,128]{1,0:T(8,128)(2,1)} %collective-permute-done.3), channel_id=1, source_target_pairs={{0,8},{8,0},{16,24},{24,16},{32,40},{40,32},{48,56},{56,48},{64,72... | collective-permute-start | bytes 393224 | tf_op jit(solution)/shard_map/ppermute | solution.py:23
  44.9 4.8 %collective-permute-start.16 = (bf16[512,128]{1,0:T(8,128)(2,1)}, bf16[512,128]{1,0:T(8,128)(2,1)}, u32[]{:S(2)}, u32[]{:S(2)}) collective-permute-start(bf16[512,128]{1,0:T(8,128)(2,1)} %collective-permute-done.4), channel_id=1, source_target_pairs={{0,8},{8,0},{16,24},{24,16},{32,40},{40,32},{48,56},{56,48},{64,72... | collective-permute-start | bytes 393224 | tf_op jit(solution)/shard_map/ppermute | solution.py:23
  44.9 5.1 %collective-permute-start.19 = (bf16[512,128]{1,0:T(8,128)(2,1)}, bf16[512,128]{1,0:T(8,128)(2,1)}, u32[]{:S(2)}, u32[]{:S(2)}) collective-permute-start(bf16[512,128]{1,0:T(8,128)(2,1)} %collective-permute-done.8), channel_id=1, source_target_pairs={{0,8},{8,0},{16,24},{24,16},{32,40},{40,32},{48,56},{56,48},{64,72... | collective-permute-start | bytes 393224 | tf_op jit(solution)/shard_map/ppermute | solution.py:23
  46.0 6.3 %collective-permute-start.12 = (bf16[512,128]{1,0:T(8,128)(2,1)}, bf16[512,128]{1,0:T(8,128)(2,1)}, u32[]{:S(2)}, u32[]{:S(2)}) collective-permute-start(bf16[512,128]{1,0:T(8,128)(2,1)} %collective-permute-done.6), channel_id=1, source_target_pairs={{0,128},{8,136},{16,144},{24,152},{32,160},{40,168},{48,176},{56,1... | collective-permute-start | bytes 393224 | tf_op jit(solution)/shard_map/ppermute | solution.py:23
  49.1 4.1 %collective-permute-start.20 = (bf16[512,128]{1,0:T(8,128)(2,1)}, bf16[512,128]{1,0:T(8,128)(2,1)}, u32[]{:S(2)}, u32[]{:S(2)}) collective-permute-start(bf16[512,128]{1,0:T(8,128)(2,1)} %collective-permute-done.9), channel_id=1, source_target_pairs={{0,8},{8,0},{16,24},{24,16},{32,40},{40,32},{48,56},{56,48},{64,72... | collective-permute-start | bytes 393224 | tf_op jit(solution)/shard_map/ppermute | solution.py:23
  49.4 3.9 %collective-permute-start.17 = (bf16[512,128]{1,0:T(8,128)(2,1)}, bf16[512,128]{1,0:T(8,128)(2,1)}, u32[]{:S(2)}, u32[]{:S(2)}) collective-permute-start(bf16[512,128]{1,0:T(8,128)(2,1)} %collective-permute-done.6), channel_id=1, source_target_pairs={{0,8},{8,0},{16,24},{24,16},{32,40},{40,32},{48,56},{56,48},{64,72... | collective-permute-start | bytes 393224 | tf_op jit(solution)/shard_map/ppermute | solution.py:23
  49.6 14.8 %collective-permute-start.22 = (bf16[784,128]{1,0:T(8,128)(2,1)}, bf16[784,128]{1,0:T(8,128)(2,1)}, u32[]{:S(2)}, u32[]{:S(2)}) collective-permute-start(bf16[784,128]{1,0:T(8,128)(2,1)} %slice.110), channel_id=1, source_target_pairs={{0,1},{1,2},{2,3},{3,0},{4,5},{5,6},{6,7},{7,4},{8,9},{9,10},{10,1... | collective-permute-start | bytes 602120 | tf_op jit(solution)/shard_map/ppermute | solution.py:27
  49.9 14.5 %collective-permute-start.23 = (bf16[784,128]{1,0:T(8,128)(2,1)}, bf16[784,128]{1,0:T(8,128)(2,1)}, u32[]{:S(2)}, u32[]{:S(2)}) collective-permute-start(bf16[784,128]{1,0:T(8,128)(2,1)} %slice.111), channel_id=1, source_target_pairs={{0,3},{1,0},{2,1},{3,2},{4,7},{5,4},{6,5},{7,6},{8,11},{9,8},{10,9... | collective-permute-start | bytes 602120 | tf_op jit(solution)/shard_map/ppermute | solution.py:27
  53.2 17.3 %collective-permute-start.25 = (bf16[1568,128]{1,0:T(8,128)(2,1)S(1)}, bf16[1568,128]{1,0:T(8,128)(2,1)S(1)}, u32[]{:S(2)}, u32[]{:S(2)}) collective-permute-start(bf16[1568,128]{1,0:T(8,128)(2,1)S(1)} %constant_dynamic-update-slice_fusion.8.refs_0_), channel_id=1, source_target_pairs={{0,8},{8,0},{16,24},{24,16},{32,40},{40,32},{48,56},{56,48},{64,72... | collective-permute-start | bytes 1204232 | tf_op jit(solution)/shard_map/ppermute | solution.py:23
  53.3 18.5 %collective-permute-start.26 = (bf16[1568,128]{1,0:T(8,128)(2,1)S(1)}, bf16[1568,128]{1,0:T(8,128)(2,1)S(1)}, u32[]{:S(2)}, u32[]{:S(2)}) collective-permute-start(bf16[1568,128]{1,0:T(8,128)(2,1)S(1)} %collective-permute-done.10.refs_1_), channel_id=1, source_target_pairs={{0,8},{8,0},{16,24},{24,16},{32,40},{40,32},{48,56},{56,48},{64,72... | collective-permute-start | bytes 1204232 | tf_op jit(solution)/shard_map/ppermute | solution.py:23
  54.5 17.3 %collective-permute-start.27 = (bf16[1568,128]{1,0:T(8,128)(2,1)S(1)}, bf16[1568,128]{1,0:T(8,128)(2,1)S(1)}, u32[]{:S(2)}, u32[]{:S(2)}) collective-permute-start(bf16[1568,128]{1,0:T(8,128)(2,1)S(1)} %collective-permute-done.11.refs_2_), channel_id=1, source_target_pairs={{0,8},{8,0},{16,24},{24,16},{32,40},{40,32},{48,56},{56,48},{64,72... | collective-permute-start | bytes 1204232 | tf_op jit(solution)/shard_map/ppermute | solution.py:23
  64.4 5.1 %collective-permute-start.24 = (bf16[256,128]{1,0:T(8,128)(2,1)S(1)}, bf16[256,128]{1,0:T(8,128)(2,1)S(1)}, u32[]{:S(2)}, u32[]{:S(2)}) collective-permute-start(bf16[256,128]{1,0:T(8,128)(2,1)S(1)} %aggregate.1), channel_id=1, source_target_pairs={{0,4},{1,5},{2,6},{3,7},{4,0},{5,1},{6,2},{7,3},{8,12},{9,13},{10,... | collective-permute-start | bytes 196616 | tf_op jit(solution)/shard_map/ppermute | solution.py:27
  67.0 3.6 %collective-permute-start.28 = (bf16[784,128]{1,0:T(8,128)(2,1)}, bf16[784,128]{1,0:T(8,128)(2,1)S(1)}, u32[]{:S(2)}, u32[]{:S(2)}) collective-permute-start(bf16[784,128]{1,0:T(8,128)(2,1)} %collective-permute-done.22.refs_3_), channel_id=1, source_target_pairs={{0,8},{8,0},{16,24},{24,16},{32,40},{40,32},{48,56},{56,48},{64,72... | collective-permute-start | bytes 602120 | tf_op jit(solution)/shard_map/ppermute | solution.py:23
  73.5 6.0 %collective-permute-start.30 = (bf16[512,128]{1,0:T(8,128)(2,1)S(1)}, bf16[512,128]{1,0:T(8,128)(2,1)S(1)}, u32[]{:S(2)}, u32[]{:S(2)}) collective-permute-start(bf16[512,128]{1,0:T(8,128)(2,1)S(1)} %pad_maximum_fusion.3.p0), channel_id=1, source_target_pairs={{0,1},{1,2},{2,3},{3,0},{4,5},{5,6},{6,7},{7,4},{8,9},{9,10},{10,1... | collective-permute-start | bytes 393224 | tf_op jit(solution)/shard_map/ppermute | solution.py:27
  74.4 5.1 %collective-permute-start.31 = (bf16[512,128]{1,0:T(8,128)(2,1)S(1)}, bf16[512,128]{1,0:T(8,128)(2,1)S(1)}, u32[]{:S(2)}, u32[]{:S(2)}) collective-permute-start(bf16[512,128]{1,0:T(8,128)(2,1)S(1)} %pad_maximum_fusion.3.p0), channel_id=1, source_target_pairs={{0,3},{1,0},{2,1},{3,2},{4,7},{5,4},{6,5},{7,6},{8,11},{9,8},{10,9... | collective-permute-start | bytes 393224 | tf_op jit(solution)/shard_map/ppermute | solution.py:27
  76.3 6.7 %collective-permute-start.32 = (bf16[512,128]{1,0:T(8,128)(2,1)S(1)}, bf16[512,128]{1,0:T(8,128)(2,1)S(1)}, u32[]{:S(2)}, u32[]{:S(2)}) collective-permute-start(bf16[512,128]{1,0:T(8,128)(2,1)S(1)} %pad_maximum_fusion.3.p0), channel_id=1, source_target_pairs={{0,2},{1,3},{2,0},{3,1},{4,6},{5,7},{6,4},{7,5},{8,10},{9,11},{10,... | collective-permute-start | bytes 393224 | tf_op jit(solution)/shard_map/ppermute | solution.py:27
  85.1 6.0 %collective-permute-start.41 = (f32[64,1152]{1,0:T(8,128)S(1)}, f32[64,1152]{1,0:T(8,128)S(1)}, u32[]{:S(2)}, u32[]{:S(2)}) collective-permute-start(f32[64,1152]{1,0:T(8,128)S(1)} %get-tuple-element.35), channel_id=1, source_target_pairs={{0,8},{8,0},{16,24},{24,16},{32,40},{40,32},{48,56},{56,48},{64,72... | collective-permute-start | bytes 884744 | tf_op jit(solution)/shard_map/ppermute | solution.py:23
  91.1 6.3 %collective-permute-start.33 = (bf16[32,128,128]{2,1,0:T(8,128)(2,1)S(1)}, bf16[32,128,128]{2,1,0:T(8,128)(2,1)S(1)}, u32[]{:S(2)}, u32[]{:S(2)}) collective-permute-start(bf16[32,128,128]{2,1,0:T(8,128)(2,1)S(1)} %get-tuple-element.32), channel_id=1, source_target_pairs={{0,8},{8,0},{16,24},{24,16},{32,40},{40,32},{48,56},{56,48},{64,72... | collective-permute-start | bytes 3145736 | tf_op jit(solution)/shard_map/ppermute | solution.py:23
  91.2 3.5 %collective-permute-start.42 = (bf16[32,1152]{1,0:T(8,128)(2,1)S(1)}, bf16[32,1152]{1,0:T(8,128)(2,1)S(1)}, u32[]{:S(2)}, u32[]{:S(2)}) collective-permute-start(bf16[32,1152]{1,0:T(8,128)(2,1)S(1)} %fusion.2), channel_id=1, source_target_pairs={{0,128},{8,136},{16,144},{24,152},{32,160},{40,168},{48,176},{56,1... | collective-permute-start | bytes 221192 | tf_op jit(solution)/shard_map/ppermute | solution.py:23
  97.9 5.0 %collective-permute-start.44 = (bf16[64,1152]{1,0:T(8,128)(2,1)S(1)}, bf16[64,1152]{1,0:T(8,128)(2,1)S(1)}, u32[]{:S(2)}, u32[]{:S(2)}) collective-permute-start(bf16[64,1152]{1,0:T(8,128)(2,1)S(1)} %pad_maximum_fusion.1), channel_id=1, source_target_pairs={{0,16},{8,120},{16,32},{24,8},{32,48},{40,24},{48,64},{56,40},{64,... | collective-permute-start | bytes 442376 | tf_op jit(solution)/shard_map/ppermute | solution.py:39
  98.0 9.0 %collective-permute-start.45 = (bf16[64,1152]{1,0:T(8,128)(2,1)S(1)}, bf16[64,1152]{1,0:T(8,128)(2,1)S(1)}, u32[]{:S(2)}, u32[]{:S(2)}) collective-permute-start(bf16[64,1152]{1,0:T(8,128)(2,1)S(1)} %pad_maximum_fusion.1), channel_id=1, source_target_pairs={{0,32},{8,104},{16,48},{24,120},{32,64},{40,8},{48,80},{56,24},{64... | collective-permute-start | bytes 442376 | tf_op jit(solution)/shard_map/ppermute | solution.py:39
  101.0 9.9 %collective-permute-start.46 = (bf16[64,1152]{1,0:T(8,128)(2,1)S(1)}, bf16[64,1152]{1,0:T(8,128)(2,1)S(1)}, u32[]{:S(2)}, u32[]{:S(2)}) collective-permute-start(bf16[64,1152]{1,0:T(8,128)(2,1)S(1)} %pad_maximum_fusion.1), channel_id=1, source_target_pairs={{0,48},{8,88},{16,64},{24,104},{32,80},{40,120},{48,96},{56,8},{64... | collective-permute-start | bytes 442376 | tf_op jit(solution)/shard_map/ppermute | solution.py:39
  101.3 9.6 %collective-permute-start.34 = (bf16[8,128,128]{2,1,0:T(8,128)(2,1)S(1)}, bf16[8,128,128]{2,1,0:T(8,128)(2,1)S(1)}, u32[]{:S(2)}, u32[]{:S(2)}) collective-permute-start(bf16[8,128,128]{2,1,0:T(8,128)(2,1)S(1)} %get-tuple-element.45), channel_id=1, source_target_pairs={{0,128},{8,136},{16,144},{24,152},{32,160},{40,168},{48,176},{56,1... | collective-permute-start | bytes 786440 | tf_op jit(solution)/shard_map/ppermute | solution.py:23
  101.9 11.4 %collective-permute-start.37 = (bf16[8,128,128]{2,1,0:T(8,128)(2,1)S(1)}, bf16[8,128,128]{2,1,0:T(8,128)(2,1)S(1)}, u32[]{:S(2)}, u32[]{:S(2)}) collective-permute-start(bf16[8,128,128]{2,1,0:T(8,128)(2,1)S(1)} %get-tuple-element.46), channel_id=1, source_target_pairs={{0,128},{8,136},{16,144},{24,152},{32,160},{40,168},{48,176},{56,1... | collective-permute-start | bytes 786440 | tf_op jit(solution)/shard_map/ppermute | solution.py:23
  113.4 20.5 %collective-permute-start.48 = (bf16[96,1152]{1,0:T(8,128)(2,1)S(1)}, bf16[96,1152]{1,0:T(8,128)(2,1)S(1)}, u32[]{:S(2)}, u32[]{:S(2)}) collective-permute-start(bf16[96,1152]{1,0:T(8,128)(2,1)S(1)} %pad_maximum_fusion), channel_id=1, source_target_pairs={{0,8},{8,0},{16,24},{24,16},{32,40},{40,32},{48,56},{56,48},{64,72... | collective-permute-start | bytes 663560 | tf_op jit(solution)/shard_map/ppermute | solution.py:23
  116.0 18.9 %collective-permute-start.38 = (bf16[4,128,128]{2,1,0:T(8,128)(2,1)S(1)}, bf16[4,128,128]{2,1,0:T(8,128)(2,1)S(1)}, u32[]{:S(2)}, u32[]{:S(2)}) collective-permute-start(bf16[4,128,128]{2,1,0:T(8,128)(2,1)S(1)} %get-tuple-element.47), channel_id=1, source_target_pairs={{0,32},{8,104},{16,48},{24,120},{32,64},{40,8},{48,80},{56,24},{64... | collective-permute-start | bytes 393224 | tf_op jit(solution)/shard_map/ppermute | solution.py:39
  118.8 16.2 %collective-permute-start.39 = (bf16[4,128,128]{2,1,0:T(8,128)(2,1)S(1)}, bf16[4,128,128]{2,1,0:T(8,128)(2,1)S(1)}, u32[]{:S(2)}, u32[]{:S(2)}) collective-permute-start(bf16[4,128,128]{2,1,0:T(8,128)(2,1)S(1)} %get-tuple-element.48), channel_id=1, source_target_pairs={{0,48},{8,88},{16,64},{24,104},{32,80},{40,120},{48,96},{56,8},{64... | collective-permute-start | bytes 393224 | tf_op jit(solution)/shard_map/ppermute | solution.py:39
  121.5 13.5 %collective-permute-start.36 = (bf16[4,128,128]{2,1,0:T(8,128)(2,1)S(1)}, bf16[4,128,128]{2,1,0:T(8,128)(2,1)S(1)}, u32[]{:S(2)}, u32[]{:S(2)}) collective-permute-start(bf16[4,128,128]{2,1,0:T(8,128)(2,1)S(1)} %slice.118), channel_id=1, source_target_pairs={{0,16},{8,120},{16,32},{24,8},{32,48},{40,24},{48,64},{56,40},{64,... | collective-permute-start | bytes 393224 | tf_op jit(solution)/shard_map/ppermute | solution.py:39
  121.6 9.4 %collective-permute-start.47 = (bf16[32,1152]{1,0:T(8,128)(2,1)S(1)}, bf16[32,1152]{1,0:T(8,128)(2,1)S(1)}, u32[]{:S(2)}, u32[]{:S(2)}) collective-permute-start(bf16[32,1152]{1,0:T(8,128)(2,1)S(1)} %fusion.4.own), channel_id=1, source_target_pairs={{0,64},{8,72},{16,80},{24,88},{32,96},{40,104},{48,112},{56,120},{... | collective-permute-start | bytes 221192 | tf_op jit(solution)/shard_map/ppermute | solution.py:23
  131.0 11.1 %collective-permute-start.35 = (bf16[2,128,128]{2,1,0:T(8,128)(2,1)S(1)}, bf16[2,128,128]{2,1,0:T(8,128)(2,1)S(1)}, u32[]{:S(2)}, u32[]{:S(2)}) collective-permute-start(bf16[2,128,128]{2,1,0:T(8,128)(2,1)S(1)} %slice.117), channel_id=1, source_target_pairs={{0,64},{8,72},{16,80},{24,88},{32,96},{40,104},{48,112},{56,120},{... | collective-permute-start | bytes 196616 | tf_op jit(solution)/shard_map/ppermute | solution.py:23
  134.6 4.0 %collective-permute-start.49 = (bf16[32,1152]{1,0:T(8,128)(2,1)S(1)}, bf16[32,1152]{1,0:T(8,128)(2,1)S(1)}, u32[]{:S(2)}, u32[]{:S(2)}) collective-permute-start(bf16[32,1152]{1,0:T(8,128)(2,1)S(1)} %sum_z.1), channel_id=1, source_target_pairs={{0,128},{8,136},{16,144},{24,152},{32,160},{40,168},{48,176},{56,1... | collective-permute-start | bytes 221192 | tf_op jit(solution)/shard_map/ppermute | solution.py:23
  135.1 7.0 %collective-permute-start.40 = (f32[2,128,128]{2,1,0:T(8,128)S(1)}, f32[2,128,128]{2,1,0:T(8,128)S(1)}, u32[]{:S(2)}, u32[]{:S(2)}) collective-permute-start(f32[2,128,128]{2,1,0:T(8,128)S(1)} %slice.124), channel_id=1, source_target_pairs={{0,8},{8,0},{16,24},{24,16},{32,40},{40,32},{48,56},{56,48},{64,72... | collective-permute-start | bytes 393224 | tf_op jit(solution)/shard_map/ppermute | solution.py:23
  138.6 4.5 %collective-permute-start.50 = (bf16[64,1152]{1,0:T(8,128)(2,1)S(1)}, bf16[64,1152]{1,0:T(8,128)(2,1)S(1)}, u32[]{:S(2)}, u32[]{:S(2)}) collective-permute-start(bf16[64,1152]{1,0:T(8,128)(2,1)S(1)} %pad_maximum_fusion.2.mine), channel_id=1, source_target_pairs={{0,8},{8,0},{16,24},{24,16},{32,40},{40,32},{48,56},{56,48},{64,72... | collective-permute-start | bytes 442376 | tf_op jit(solution)/shard_map/ppermute | solution.py:23
  (17 other events, 194.1 us)
